TPU v7x, 32 devices: a whole 2x2x4 slice. The times are simulated.
32 devices in a mesh: row: 8 (over z, y), col: 4 (over x, core).
Axes of the slice: x: 2, y: 2, z: 4, core: 2. Of those that a mesh axis runs over, the one named last changes fastest.
Arguments:
- hidden_act: bfloat16 [768, 26624], P('col', 'row'), may hold values from -6 to 6
- out_grad: bfloat16 [768, 16384], P('row', 'col'), may hold values from -6 to 6
- down_weight: bfloat16 [26624, 16384], P('row', 'col'), may hold values from -0.046875 to 0.046875
Outputs:
- fisher: float32 [26624, 16384], P('row', 'col')
- hidden_grad: bfloat16 [768, 26624], P('col', 'row')
All inputs are finite; a program needn't handle non-finite values.
Results may differ from a plain program's by a relative error of at most 0.001.
Values may be sent and summed in bfloat16 or wider, within the bound.
No kernel may reach another device: no remote copies, remote signals or barrier semaphores. Data moves between devices by JAX's collectives and lax.ppermute only.
A program may use at most 192 MiB of HBM per device.

v0:
```python
import jax
import jax.numpy as jnp
from jax import lax
from jax.sharding import PartitionSpec as P

SEQ = 96
EXAMPLES = 8


def per_device(hidden_act, out_grad, down_weight):
    act_whole = lax.all_gather(hidden_act, "col", axis=0, tiled=True)
    grad_whole = lax.all_gather(out_grad, "row", axis=0, tiled=True)
    feat_rows = down_weight.shape[0]
    feat_cols = down_weight.shape[1]

    def accumulate(example, total):
        start = (example * SEQ).astype(jnp.int32)
        act_piece = lax.dynamic_slice_in_dim(act_whole, start, SEQ, 0)
        grad_piece = lax.dynamic_slice_in_dim(grad_whole, start, SEQ, 0)
        grad_e = lax.dot_general(
            act_piece, grad_piece, (((0,), (0,)), ((), ())), preferred_element_type=jnp.float32
        )
        return total + grad_e * grad_e

    total = lax.fori_loop(0, EXAMPLES, accumulate, jnp.zeros((feat_rows, feat_cols), jnp.float32))
    fisher = total / (EXAMPLES * SEQ)
    summed = lax.psum_scatter(
        lax.dot_general(
            grad_whole, down_weight, (((1,), (1,)), ((), ())), preferred_element_type=jnp.float32
        ),
        "col",
        scatter_dimension=0,
        tiled=True,
    )
    return (fisher, summed.astype(jnp.bfloat16))


def solution(mesh):
    placed = (P("col", "row"), P("row", "col"), P("row", "col"))
    return jax.shard_map(
        per_device,
        mesh=mesh,
        in_specs=placed,
        out_specs=(P("row", "col"), P("col", "row")),
        check_vma=False,
    )
```

profile of v0, /device:TPU:0, one launch (start us, length us, event | category | flops | bytes accessed | tf_op | source)
XLA Modules:
  0.0 478.3 jit_solution(6444310962151930377)
XLA Ops:
  7.2 0.0 all-gather.5.cloned.1.call-start
  7.2 0.7 all-gather.5.cloned.1.call-update
  7.9 0.0 all-gather.3.cloned.1.call-start
  7.9 0.7 all-gather.3.cloned.1.call-update
  8.6 0.0 reduce-scatter.2.cloned.1.call-start
  8.7 102.9 %all-gather.5.cloned.1.call-done = bf16[768,4096]{1,0:T(8,128)(2,1)} async-done(((bf16[96,4096]{1,0:T(8,128)(2,1)}), bf16[768,4096]{1,0:T(8,128)(2,1)}) %all-gather.5.cloned.1.call-update) | async-done | bytes 6291472 | tf_op jit(solution)/shard_map/all_gather | solution.py:12
  111.6 29.3 %fusion.3 = f32[768,3328]{1,0:T(8,128)} fusion(bf16[768,4096]{1,0:T(8,128)(2,1)} %all-gather.5.cloned.1.call-done, bf16[3328,4096]{1,0:T(8,128)(2,1)} %param.7), kind=kOutput, calls=%fused_computation.5 | convolution fusion | flops 20937965568 | bytes 43778048 | tf_op jit(solution)/shard_map/dot_general | solution.py:28
  140.9 0.0 reduce-scatter.2.cloned.1.call-update
  140.9 10.1 %all-gather.3.cloned.1.call-done = bf16[768,3328]{1,0:T(8,128)(2,1)} async-done(((bf16[192,3328]{1,0:T(8,128)(2,1)}), bf16[768,3328]{1,0:T(8,128)(2,1)}) %all-gather.3.cloned.1.call-update) | async-done | bytes 5111824 | tf_op jit(solution)/shard_map/all_gather | solution.py:11
  151.0 282.1 %while.14 = (s32[]{:T(128)}, f32[3328,4096]{1,0:T(8,128)}, bf16[768,3328]{1,0:T(8,128)(2,1)}, bf16[768,4096]{1,0:T(8,128)(2,1)}, s32[]{:T(128)}, /*index=5*/s32[]{:T(128)}, s32[]{:T(128)}, s32[]{:T(128)}) while((s32[]{:T(128)}, f32[3328,4096]{1,0:T(8,128)}, bf16[768,3328]{1,0:T(8,128)(2,1)}, bf16[768,4096]{1,0:T(8,128)(2,1)}, ...), condition=%wide.region_1.0_spmd.clone, body=%wide.region_0.0_spmd.clone.sunk | while | flops 2658140160 | bytes 110478984 | solution.py:25
  151.0 25.6 %select_add_fusion.2 = f32[3328,4096]{1,0:T(8,128)} fusion(f32[3328,4096]{1,0:T(8,128)} %get-tuple-element.139, pred[]{:T(512)S(6)} %compare.3, bf16[768,4096]{1,0:T(8,128)(2,1)} %get-tuple-element.149, s32[]{:T(128)S(6)} %select_n.10, bf16[768,3328]{1,0:T(8,128)(2,1)} %get-tuple-element.148), kind=kOutput, calls=%fused_computation.clone.1 | convolution fusion | flops 2658140160 | bytes 110478848 | tf_op jit(solution)/shard_map/while/body/eval_jaxpr/dot_general | solution.py:20
  176.7 38.3 %select_add_fusion.2 = f32[3328,4096]{1,0:T(8,128)} fusion(f32[3328,4096]{1,0:T(8,128)} %get-tuple-element.139, pred[]{:T(512)S(6)} %compare.3, bf16[768,4096]{1,0:T(8,128)(2,1)} %get-tuple-element.149, s32[]{:T(128)S(6)} %select_n.10, bf16[768,3328]{1,0:T(8,128)(2,1)} %get-tuple-element.148), kind=kOutput, calls=%fused_computation.clone.1 | convolution fusion | flops 2658140160 | bytes 110478848 | tf_op jit(solution)/shard_map/while/body/eval_jaxpr/dot_general | solution.py:20
  215.0 36.6 %select_add_fusion.2 = f32[3328,4096]{1,0:T(8,128)} fusion(f32[3328,4096]{1,0:T(8,128)} %get-tuple-element.139, pred[]{:T(512)S(6)} %compare.3, bf16[768,4096]{1,0:T(8,128)(2,1)} %get-tuple-element.149, s32[]{:T(128)S(6)} %select_n.10, bf16[768,3328]{1,0:T(8,128)(2,1)} %get-tuple-element.148), kind=kOutput, calls=%fused_computation.clone.1 | convolution fusion | flops 2658140160 | bytes 110478848 | tf_op jit(solution)/shard_map/while/body/eval_jaxpr/dot_general | solution.py:20
  251.6 36.3 %select_add_fusion.2 = f32[3328,4096]{1,0:T(8,128)} fusion(f32[3328,4096]{1,0:T(8,128)} %get-tuple-element.139, pred[]{:T(512)S(6)} %compare.3, bf16[768,4096]{1,0:T(8,128)(2,1)} %get-tuple-element.149, s32[]{:T(128)S(6)} %select_n.10, bf16[768,3328]{1,0:T(8,128)(2,1)} %get-tuple-element.148), kind=kOutput, calls=%fused_computation.clone.1 | convolution fusion | flops 2658140160 | bytes 110478848 | tf_op jit(solution)/shard_map/while/body/eval_jaxpr/dot_general | solution.py:20
  287.9 36.3 %select_add_fusion.2 = f32[3328,4096]{1,0:T(8,128)} fusion(f32[3328,4096]{1,0:T(8,128)} %get-tuple-element.139, pred[]{:T(512)S(6)} %compare.3, bf16[768,4096]{1,0:T(8,128)(2,1)} %get-tuple-element.149, s32[]{:T(128)S(6)} %select_n.10, bf16[768,3328]{1,0:T(8,128)(2,1)} %get-tuple-element.148), kind=kOutput, calls=%fused_computation.clone.1 | convolution fusion | flops 2658140160 | bytes 110478848 | tf_op jit(solution)/shard_map/while/body/eval_jaxpr/dot_general | solution.py:20
  324.2 36.3 %select_add_fusion.2 = f32[3328,4096]{1,0:T(8,128)} fusion(f32[3328,4096]{1,0:T(8,128)} %get-tuple-element.139, pred[]{:T(512)S(6)} %compare.3, bf16[768,4096]{1,0:T(8,128)(2,1)} %get-tuple-element.149, s32[]{:T(128)S(6)} %select_n.10, bf16[768,3328]{1,0:T(8,128)(2,1)} %get-tuple-element.148), kind=kOutput, calls=%fused_computation.clone.1 | convolution fusion | flops 2658140160 | bytes 110478848 | tf_op jit(solution)/shard_map/while/body/eval_jaxpr/dot_general | solution.py:20
  360.5 36.3 %select_add_fusion.2 = f32[3328,4096]{1,0:T(8,128)} fusion(f32[3328,4096]{1,0:T(8,128)} %get-tuple-element.139, pred[]{:T(512)S(6)} %compare.3, bf16[768,4096]{1,0:T(8,128)(2,1)} %get-tuple-element.149, s32[]{:T(128)S(6)} %select_n.10, bf16[768,3328]{1,0:T(8,128)(2,1)} %get-tuple-element.148), kind=kOutput, calls=%fused_computation.clone.1 | convolution fusion | flops 2658140160 | bytes 110478848 | tf_op jit(solution)/shard_map/while/body/eval_jaxpr/dot_general | solution.py:20
  396.8 36.3 %select_add_fusion.2 = f32[3328,4096]{1,0:T(8,128)} fusion(f32[3328,4096]{1,0:T(8,128)} %get-tuple-element.139, pred[]{:T(512)S(6)} %compare.3, bf16[768,4096]{1,0:T(8,128)(2,1)} %get-tuple-element.149, s32[]{:T(128)S(6)} %select_n.10, bf16[768,3328]{1,0:T(8,128)(2,1)} %get-tuple-element.148), kind=kOutput, calls=%fused_computation.clone.1 | convolution fusion | flops 2658140160 | bytes 110478848 | tf_op jit(solution)/shard_map/while/body/eval_jaxpr/dot_general | solution.py:20
  433.1 35.8 %broadcast_multiply_fusion = f32[3328,4096]{1,0:T(8,128)} fusion(f32[3328,4096]{1,0:T(8,128)} %get-tuple-element.81), kind=kLoop, calls=%fused_computation.4 | loop fusion | flops 13631488 | bytes 109051904 | tf_op jit(solution)/shard_map/div | solution.py:26
  468.9 0.0 reduce-scatter.2.cloned.1.call-done
  468.9 2.9 convert_element_type.3
  (1 shorter events, 0.0 us)
Async XLA Ops:
  7.2 104.4 %all-gather.5.cloned.1.call-start = ((), (), s32[]{:S(2)}) async-start(), calls=%async_computation.2 | async-start | bytes 7077888 | tf_op jit(solution)/shard_map/all_gather | solution.py:12
  7.9 143.1 %all-gather.3.cloned.1.call-start = ((), (), s32[]{:S(2)}) async-start(), calls=%async_computation.1 | async-start | bytes 6389760 | tf_op jit(solution)/shard_map/all_gather | solution.py:11
  8.6 460.2 %reduce-scatter.2.cloned.1.call-start = ((), (), s32[]{:S(2)}) async-start(), calls=%async_computation.3 | async-start | bytes 12779520 | tf_op jit(solution)/shard_map/reduce_scatter | solution.py:27
Sparse Core Ops, SparseCore 0:
  10.2 101.4 all-gather.4
  113.2 37.8 all-gather.2
  153.7 82.7 reduce-scatter.1
where the time goes:
time: 478 us
  matrix products  311 us (65%)
  waiting for transfers between devices  114 us (24%)
  other arithmetic  38.7 us (8%)
  between operations  13.8 us (3%)
    dot_general x8, matrix products, accumulate(): lax.dot_general(act_piece, grad_piece, (((0,), (0,)), ((), ())), preferre...  282 us
    all_gather x1, waiting for transfers between devices, per_device(): grad_whole = lax.all_gather(out_grad, 'row', axis=0, tiled=True)  103 us
    div x1, other arithmetic, per_device(): fisher = total / (EXAMPLES * SEQ)  35.8 us
    dot_general x1, matrix products, per_device(): lax.dot_general(grad_whole, down_weight, (((1,), (1,)), ((), ())), prefer...  29.3 us
    all_gather x1, waiting for transfers between devices, per_device(): act_whole = lax.all_gather(hidden_act, 'col', axis=0, tiled=True)  10.1 us
  transfers between devices with their start and end apart: 3, of which 2 were waited for; matrix products, arithmetic and copies ran while one was open for 73% of the time, Pallas kernels for 0%

commit v1 on v0

v1 whole, which is shorter than its diff:
```python
import functools

import jax
import jax.numpy as jnp
from jax import lax
from jax.experimental import pallas as pl
from jax.experimental.pallas import tpu as pltpu
from jax.sharding import PartitionSpec as P

SEQ = 96
EXAMPLES = 8
LANES = 128


def largest_block(size, limit):
    return max(b for b in range(LANES, limit + 1, LANES) if size % b == 0)


def fisher_kernel(act_ref, grad_ref, out_ref, rows_ref, *, width):
    depth = rows_ref.shape[1] // EXAMPLES
    columns = out_ref.shape[1]

    for e in range(EXAMPLES):
        piece = act_ref[e * SEQ : (e + 1) * SEQ, :]
        rows_ref[:, e * depth : e * depth + SEQ] = piece.T

    for j in range(0, columns, width):
        total = None
        for e in range(EXAMPLES):
            grad_e = lax.dot_general(
                rows_ref[:, e * depth : e * depth + SEQ],
                grad_ref[e * SEQ : (e + 1) * SEQ, j : j + width],
                (((1,), (0,)), ((), ())),
                preferred_element_type=jnp.float32,
            )
            total = grad_e * grad_e if total is None else total + grad_e * grad_e
        out_ref[:, j : j + width] = total * (1.0 / (EXAMPLES * SEQ))


def fisher_of(act, grad):
    tokens, rows = act.shape
    columns = grad.shape[1]
    block = largest_block(rows, 256)
    width = largest_block(columns, 256)
    return pl.pallas_call(
        functools.partial(fisher_kernel, width=width),
        out_shape=jax.ShapeDtypeStruct((rows, columns), jnp.float32),
        grid=(rows // block,),
        in_specs=[
            pl.BlockSpec((tokens, block), lambda i: (0, i)),
            pl.BlockSpec((tokens, columns), lambda i: (0, 0), pipeline_mode=pl.Buffered(1)),
        ],
        out_specs=pl.BlockSpec((block, columns), lambda i: (i, 0)),
        scratch_shapes=[pltpu.VMEM((block, EXAMPLES * LANES), act.dtype)],
        cost_estimate=pl.CostEstimate(
            flops=2 * tokens * rows * columns,
            bytes_accessed=4 * rows * columns + 2 * tokens * (rows + columns),
            transcendentals=0,
        ),
        compiler_params=pltpu.CompilerParams(dimension_semantics=("arbitrary",)),
        name="fisher",
    )(act, grad)


def per_device(hidden_act, out_grad, down_weight):
    grad_whole = lax.all_gather(out_grad, "row", axis=0, tiled=True)
    act_whole = lax.all_gather(hidden_act, "col", axis=0, tiled=True)
    summed = lax.psum_scatter(
        lax.dot_general(
            grad_whole, down_weight, (((1,), (1,)), ((), ())), preferred_element_type=jnp.float32
        ),
        "col",
        scatter_dimension=0,
        tiled=True,
    )
    return (fisher_of(act_whole, grad_whole), summed.astype(jnp.bfloat16))


def solution(mesh):
    placed = (P("col", "row"), P("row", "col"), P("row", "col"))
    return jax.shard_map(
        per_device,
        mesh=mesh,
        in_specs=placed,
        out_specs=(P("row", "col"), P("col", "row")),
        check_vma=False,
    )
```

time: 478 us -> 246 us (0.51)
  matrix products: 311 us -> 29.3 us
  Pallas kernels: 0 us -> 65.1 us
  other arithmetic: 38.7 us -> 2.89 us
  waiting for transfers between devices: 114 us -> 135 us
    dot_general x8 -> x0, matrix products: 282 us -> none  [accumulate(): lax.dot_general(act_piece, grad_piece, (((0,), (0,)), ((), ())), preferre...]
    pallas_call x0 -> x1, Pallas kernels: none -> 65.1 us  [fisher_of(): pl.pallas_call(functools.partial(fisher_kernel, width=width), out_shape=j...]
    div x1 -> x0, other arithmetic: 35.8 us -> none  [per_device(): fisher = total / (EXAMPLES * SEQ)]
    reduce_scatter x1, waiting for transfers between devices: 0.01 us -> 20.3 us  [per_device(): lax.psum_scatter(lax.dot_general(grad_whole, down_weight, (((1,), (1,)),...]
  transfers between devices with their start and end apart: 3 -> 3, of which waited for: 2 -> 3; matrix products, arithmetic and copies ran while one was open for 73% -> 12% of each run, Pallas kernels for 0% -> 26%
where the time goes in v1:
time: 246 us
  waiting for transfers between devices  135 us (55%)
  Pallas kernels  65.1 us (26%)
  matrix products  29.3 us (12%)
  between operations  13.7 us (6%)
  other arithmetic  2.89 us (1%)
    all_gather x1, waiting for transfers between devices, per_device(): grad_whole = lax.all_gather(out_grad, 'row', axis=0, tiled=True)  103 us
    pallas_call x1, Pallas kernels, fisher_of(): pl.pallas_call(functools.partial(fisher_kernel, width=width), out_shape=j...  65.1 us
    dot_general x1, matrix products, per_device(): lax.dot_general(grad_whole, down_weight, (((1,), (1,)), ((), ())), prefer...  29.3 us
    reduce_scatter x1, waiting for transfers between devices, per_device(): lax.psum_scatter(lax.dot_general(grad_whole, down_weight, (((1,), (1,)),...  20.3 us
    all_gather x1, waiting for transfers between devices, per_device(): act_whole = lax.all_gather(hidden_act, 'col', axis=0, tiled=True)  10.1 us
  transfers between devices with their start and end apart: 3, of which 3 were waited for; matrix products, arithmetic and copies ran while one was open for 12% of the time, Pallas kernels for 26%

profile of v1, /device:TPU:0, one launch (start us, length us, event | category | flops | bytes accessed | tf_op | source)
XLA Modules:
  0.0 245.9 jit_solution(2421872378603778670)
XLA Ops:
  7.2 0.0 all-gather.5.cloned.1.call-start
  7.2 0.7 all-gather.5.cloned.1.call-update
  7.9 0.0 all-gather.3.cloned.1.call-start
  7.9 0.7 all-gather.3.cloned.1.call-update
  8.6 0.0 reduce-scatter.2.cloned.1.call-start
  8.7 102.9 %all-gather.5.cloned.1.call-done.grad_ref = bf16[768,4096]{1,0:T(8,128)(2,1)} async-done(((bf16[96,4096]{1,0:T(8,128)(2,1)}), bf16[768,4096]{1,0:T(8,128)(2,1)}) %all-gather.5.cloned.1.call-update) | async-done | bytes 6291472 | tf_op jit(solution)/shard_map/all_gather | solution.py:66
  111.6 29.3 %fusion = f32[768,3328]{1,0:T(8,128)} fusion(bf16[768,4096]{1,0:T(8,128)(2,1)} %all-gather.5.cloned.1.call-done.grad_ref, bf16[3328,4096]{1,0:T(8,128)(2,1)} %param.5), kind=kOutput, calls=%fused_computation | convolution fusion | flops 20937965568 | bytes 43778048 | tf_op jit(solution)/shard_map/dot_general | solution.py:69
  140.9 0.0 reduce-scatter.2.cloned.1.call-update
  140.9 10.1 %all-gather.3.cloned.1.call-done.act_ref = bf16[768,3328]{1,0:T(8,128)(2,1)} async-done(((bf16[192,3328]{1,0:T(8,128)(2,1)}), bf16[768,3328]{1,0:T(8,128)(2,1)}) %all-gather.3.cloned.1.call-update) | async-done | bytes 5111824 | tf_op jit(solution)/shard_map/all_gather | solution.py:67
  151.0 65.1 %fisher.1 = f32[3328,4096]{1,0:T(8,128)} custom-call(bf16[768,3328]{1,0:T(8,128)(2,1)} %all-gather.3.cloned.1.call-done.act_ref, bf16[768,4096]{1,0:T(8,128)(2,1)} %all-gather.5.cloned.1.call-done.grad_ref), custom_call_target="tpu_custom_call" | custom-call | flops 20937965568 | bytes 65929216 | tf_op jit(solution)/shard_map/fisher/pallas_call | solution.py:45
  216.2 20.3 %reduce-scatter.2.cloned.1.call-done = f32[192,3328]{1,0:T(8,128)} async-done(((f32[768,3328]{1,0:T(8,128)}), f32[192,3328]{1,0:T(8,128)}) %reduce-scatter.2.cloned.1.call-update) | async-done | bytes 2555920 | tf_op jit(solution)/shard_map/reduce_scatter | solution.py:68
  236.5 2.9 %convert_element_type.3 = bf16[192,3328]{1,0:T(8,128)(2,1)} convert(f32[192,3328]{1,0:T(8,128)} %reduce-scatter.2.cloned.1.call-done) | non-fusion elementwise | flops 638976 | bytes 3833856 | tf_op jit(solution)/shard_map/convert_element_type | solution.py:76
Async XLA Ops:
  7.2 104.4 %all-gather.5.cloned.1.call-start = ((), (), s32[]{:S(2)}) async-start(), calls=%async_computation.2 | async-start | bytes 7077888 | tf_op jit(solution)/shard_map/all_gather | solution.py:66
  7.9 143.1 %all-gather.3.cloned.1.call-start = ((), (), s32[]{:S(2)}) async-start(), calls=%async_computation.1 | async-start | bytes 6389760 | tf_op jit(solution)/shard_map/all_gather | solution.py:67
  8.6 227.8 %reduce-scatter.2.cloned.1.call-start = ((), (), s32[]{:S(2)}) async-start(), calls=%async_computation.3 | async-start | bytes 12779520 | tf_op jit(solution)/shard_map/reduce_scatter | solution.py:68
Sparse Core Ops, SparseCore 0:
  10.2 101.4 all-gather.4
  113.2 37.8 all-gather.2
  153.7 82.7 reduce-scatter.1

commit v2 on v1

v2 whole, which is shorter than its diff:
```python
import functools

import jax
import jax.numpy as jnp
import numpy as np
from jax import lax
from jax.experimental import pallas as pl
from jax.experimental.pallas import tpu as pltpu
from jax.sharding import PartitionSpec as P


SEQ = 96
EXAMPLES = 8
LANES = 128
EIGHTHS = (3, 5)
SPLITS = 3
BUFFERS = 4
POWER_TOP = 2.0**7.75

F32 = jnp.float32
ROWS_BY_ROWS = (((1,), (1,)), ((), ()))
ROWS_BY_COLUMNS = (((1,), (0,)), ((), ()))


def largest_block(size, limit):
    return max(b for b in range(LANES, limit + 1, LANES) if size % b == 0)


def params(mib=None):
    limit = {} if mib is None else {"vmem_limit_bytes": mib << 20}
    return pltpu.CompilerParams(dimension_semantics=("arbitrary",), **limit)


def in_vmem():
    return pl.BlockSpec(memory_space=pltpu.VMEM)


def turn_kernel(*refs, slot, step):
    act_refs, rows_ref = refs[:2], refs[-1]
    for act_ref in act_refs:
        for row in range(0, act_ref.shape[0], SEQ):
            for units in range(0, act_ref.shape[1], step):
                rows_ref[slot, units : units + step, :SEQ] = act_ref[
                    row : row + SEQ, units : units + step
                ].T
            slot += 1


def turned(acts, held, slot):
    units = acts[0].shape[1]
    return pl.pallas_call(
        functools.partial(turn_kernel, slot=slot, step=largest_block(units, 256)),
        out_shape=jax.ShapeDtypeStruct((EXAMPLES, units, LANES), acts[0].dtype),
        in_specs=[in_vmem()] * (2 + len(held)),
        out_specs=in_vmem(),
        input_output_aliases={2: 0} if held else {},
        cost_estimate=pl.CostEstimate(
            flops=4 * acts[0].size, bytes_accessed=8 * acts[0].size, transcendentals=0
        ),
        compiler_params=pltpu.CompilerParams(vmem_limit_bytes=16 << 20),
    )(*acts, *held)


def fisher_kernel(at_ref, rows_ref, *refs, width, part, block, first, blocks, start):
    grad_refs = refs[:EXAMPLES]
    fisher_ref, out_ref, sems = refs[-3:]
    parts = grad_refs[0].shape[1] // part

    def units(i):
        return pl.ds(pl.multiple_of((first + i) * block, block), block)

    def sending(i, n):
        return pltpu.make_async_copy(
            out_ref.at[n], fisher_ref.at[units(i), pl.ds(start + n * part, part)], sems.at[n]
        )

    def one_block(i, carry):
        for n in range(parts):

            @pl.when(i > 0)
            def _():
                sending(i - 1, n).wait()

            for j in range(0, part, width):
                total = None
                for s, grad_ref in enumerate(grad_refs):
                    grad_e = lax.dot_general(
                        rows_ref[at_ref[s], units(i), :SEQ],
                        grad_ref[:, n * part + j : n * part + j + width],
                        ROWS_BY_COLUMNS,
                        preferred_element_type=F32,
                    )
                    total = grad_e * grad_e if total is None else total + grad_e * grad_e
                out_ref[n, :, j : j + width] = total * (1.0 / (EXAMPLES * SEQ))
            sending(i, n).start()
        return carry

    lax.fori_loop(0, blocks, one_block, 0)
    for n in range(parts):
        sending(blocks - 1, n).wait()


def row_block(units):
    return max(b for b in range(16, 417, 16) if units % b == 0)


def fisher_part(at, rows, grads, held, shape, first, blocks, start):
    block = row_block(shape[0])
    columns = grads[0].shape[1]
    part = largest_block(columns, columns // 2)
    in_specs = [pl.BlockSpec(memory_space=pltpu.SMEM)] + [in_vmem()] * (1 + len(grads))
    operands = [at, rows, *grads]
    aliases = {}
    if held is not None:
        aliases = {len(operands): 0}
        operands.append(held)
        in_specs.append(pl.BlockSpec(memory_space=pl.ANY))
    tokens = EXAMPLES * SEQ
    return pl.pallas_call(
        functools.partial(
            fisher_kernel,
            width=largest_block(part, 256),
            part=part,
            block=block,
            first=first,
            blocks=blocks,
            start=start,
        ),
        out_shape=jax.ShapeDtypeStruct(shape, F32),
        in_specs=in_specs,
        out_specs=pl.BlockSpec(memory_space=pl.ANY),
        scratch_shapes=[
            pltpu.VMEM((columns // part, block, part), F32),
            pltpu.SemaphoreType.DMA((columns // part,)),
        ],
        input_output_aliases=aliases,
        cost_estimate=pl.CostEstimate(
            flops=5 * tokens * blocks * block * columns,
            bytes_accessed=4 * blocks * block * columns,
            transcendentals=0,
        ),
        compiler_params=pltpu.CompilerParams(vmem_limit_bytes=16 << 20),
    )(*operands)


def hidden_kernel(to_ref, *refs, places, block, start):
    grad_refs, weight_ref = refs[:EXAMPLES], refs[EXAMPLES]
    held_refs, out_refs = refs[EXAMPLES + 1 : -3 - places], refs[-3 - places : -3]
    tokens_ref, buffer_ref, sems = refs[-3:]
    columns = grad_refs[0].shape[1]
    blocks = weight_ref.shape[0] // block

    def units(i):
        return pl.ds(pl.multiple_of(i * block, block), block)

    def fetching(i):
        slot = lax.rem(i, BUFFERS)
        return pltpu.make_async_copy(
            weight_ref.at[units(i), pl.ds(start, columns)], buffer_ref.at[slot], sems.at[slot]
        )

    for i in range(min(BUFFERS - 1, blocks)):
        fetching(jnp.int32(i)).start()
    for s in range(EXAMPLES):
        tokens_ref[to_ref[s]] = grad_refs[s][...]

    def one_block(i, carry):
        @pl.when(i + BUFFERS - 1 < blocks)
        def _():
            fetching(i + BUFFERS - 1).start()

        fetching(i).wait()
        tokens = tokens_ref[...].reshape(EXAMPLES * SEQ, columns)
        part = lax.dot_general(
            tokens, buffer_ref[lax.rem(i, BUFFERS)], ROWS_BY_ROWS, preferred_element_type=F32
        )
        rows = part.shape[0] // places
        for n, out_ref in enumerate(out_refs):
            piece = part[n * rows : (n + 1) * rows]
            out_ref[:, units(i)] = piece + held_refs[n][:, units(i)] if held_refs else piece
        return carry

    lax.fori_loop(0, blocks, one_block, 0)


def hidden_part(to, grads, weight, held, places, start):
    units = weight.shape[0]
    columns = grads[0].shape[1]
    block = largest_block(units, 256)
    rows = EXAMPLES * SEQ // places
    return pl.pallas_call(
        functools.partial(hidden_kernel, places=places, block=block, start=start),
        out_shape=[jax.ShapeDtypeStruct((rows, units), F32)] * places,
        in_specs=[pl.BlockSpec(memory_space=pltpu.SMEM)]
        + [in_vmem()] * EXAMPLES
        + [pl.BlockSpec(memory_space=pl.ANY)]
        + [in_vmem()] * len(held),
        out_specs=[in_vmem()] * places,
        scratch_shapes=[
            pltpu.VMEM((EXAMPLES, SEQ, columns), weight.dtype),
            pltpu.VMEM((BUFFERS, block, columns), weight.dtype),
            pltpu.SemaphoreType.DMA((BUFFERS,)),
        ],
        input_output_aliases={2 + EXAMPLES + n: n for n in range(len(held))},
        cost_estimate=pl.CostEstimate(
            flops=2 * EXAMPLES * SEQ * units * columns,
            bytes_accessed=2 * units * columns,
            transcendentals=0,
        ),
        compiler_params=pltpu.CompilerParams(vmem_limit_bytes=28 << 20),
    )(to, *grads, weight, *held)


def encode_kernel(a_ref, b_ref, code_ref):
    total = a_ref[...] + b_ref[...]
    units = total.shape[1]
    top = jnp.maximum(jnp.max(jnp.abs(total), axis=1, keepdims=True), 1e-35) * 1.004
    scale = jnp.broadcast_to(top, (total.shape[0], LANES)).astype(code_ref.dtype)
    code_ref[:, units:] = scale
    share = total * (POWER_TOP / scale.astype(F32)[:, :1])
    power = share * share
    power = power * power
    power = power * power
    power = power * power
    code_ref[:, :units] = jnp.where(share < 0, -power, power).astype(code_ref.dtype)


def decode_kernel(*refs):
    mine_ref, other_ref, code_refs, out_ref = refs[0], refs[1], refs[2:-1], refs[-1]
    total = mine_ref[...] + other_ref[...]
    units = total.shape[1]
    for code_ref in code_refs:
        power = code_ref[:, :units].astype(F32)
        root = jnp.exp(jnp.log(jnp.abs(power)) * (1.0 / 16))
        scale = code_ref[:, units:].astype(F32)[:, :1] * (1.0 / POWER_TOP)
        total = total + jnp.where(power < 0, -root, root) * scale
    out_ref[...] = total.astype(out_ref.dtype)


def by_rows(kernel, out_columns, dtype, *arrays):
    rows = arrays[0].shape[0]
    block = 48 if rows % 48 == 0 else rows
    return pl.pallas_call(
        kernel,
        out_shape=jax.ShapeDtypeStruct((rows, out_columns), dtype),
        grid=(rows // block,),
        in_specs=[pl.BlockSpec((block, a.shape[1]), lambda i: (i, 0)) for a in arrays],
        out_specs=pl.BlockSpec((block, out_columns), lambda i: (i, 0)),
        cost_estimate=pl.CostEstimate(
            flops=10 * rows * out_columns, bytes_accessed=8 * rows * out_columns, transcendentals=0
        ),
        compiler_params=params(20),
    )(*arrays)


def ring_places(size):
    return list(range(0, size, 2)) + list(range(size - 1, 0, -2))


def ring_gather(piece, size):
    ring = ring_places(size)
    right = [(ring[n], ring[(n + 1) % size]) for n in range(size)]
    left = [(b, a) for a, b in right]
    found, from_left, from_right = [piece], piece, piece
    for step in range(1, size // 2 + 1):
        from_left = lax.ppermute(from_left, "row", right)
        found.append(from_left)
        if step < size - size // 2:
            from_right = lax.ppermute(from_right, "row", left)
            found.append(from_right)
    return found


def ring_rows(size):
    steps = [0]
    for step in range(1, size // 2 + 1):
        steps.append(size - step)
        if step < size - size // 2:
            steps.append(step)
    row = lax.axis_index("row").astype(jnp.uint32)
    mine = jnp.where(row % 2 == 0, row // 2, size - 1 - row // 2)
    places = (mine + np.array(steps, np.uint32)) % size
    return jnp.where(places < size // 2, 2 * places, 2 * (size - 1 - places) + 1)


def pipelined(hidden_act, out_grad, down_weight, row_size, col_size):
    chips = col_size // 2
    units, features = down_weight.shape
    per_col = hidden_act.shape[0] // SEQ
    other_core = [(c, c ^ 1) for c in range(col_size)]
    ahead = {
        d: [(c, (c + 2 * d) % col_size) for c in range(col_size)] for d in range(1, chips)
    }

    acts = []
    for d in range(chips):
        same = hidden_act
        if d > 0:
            same = lax.ppermute(hidden_act, "col", ahead[d])
        acts += [same, lax.ppermute(same, "col", other_core)]

    edges = [features * sum(EIGHTHS[:p]) // 8 for p in range(len(EIGHTHS) + 1)]
    grads = [ring_gather(out_grad[:, a:b], row_size) for a, b in zip(edges, edges[1:])]

    examples = ring_rows(row_size)
    col = lax.axis_index("col").astype(jnp.uint32)
    owner = examples // per_col
    core = (owner ^ col) & 1
    behind = (col // 2 + chips - owner // 2) % chips
    at = ((behind * 2 + core) * per_col + examples % per_col).astype(jnp.int32)
    before = (owner // 2 + 2 * chips - 1 - col // 2) % chips
    to = ((before * 2 + 1 - core) * per_col + examples % per_col).astype(jnp.int32)

    rows = ()
    for d in range(chips):
        rows = (turned(acts[2 * d : 2 * d + 2], rows, 2 * d * per_col),)
    shape = (units, features)
    blocks = units // row_block(units)
    cuts = [blocks * n // SPLITS for n in range(SPLITS + 1)]
    fisher, sums = None, []
    for p, start in enumerate(edges[:-1]):
        sums = hidden_part(to, grads[p], down_weight, sums, 2 * chips, start)
        for a, b in zip(cuts, cuts[1:]):
            fisher = fisher_part(at, rows[0], grads[p], fisher, shape, a, b - a, start)
    codes = []
    for d in range(1, chips):
        given = lax.ppermute(sums[2 * d - 2], "col", other_core)
        code = by_rows(encode_kernel, units + LANES, jnp.bfloat16, sums[2 * d - 1], given)
        codes.append(lax.ppermute(code, "col", ahead[d]))
    given = lax.ppermute(sums[-2], "col", other_core)
    return fisher, by_rows(decode_kernel, units, jnp.bfloat16, sums[-1], given, *codes)


def whole_kernel(act_ref, grad_ref, out_ref, rows_ref, *, width):
    for e in range(EXAMPLES):
        rows_ref[e, :, :SEQ] = act_ref[e * SEQ : (e + 1) * SEQ, :].T
    for j in range(0, out_ref.shape[1], width):
        total = None
        for e in range(EXAMPLES):
            grad_e = lax.dot_general(
                rows_ref[e, :, :SEQ],
                grad_ref[e * SEQ : (e + 1) * SEQ, j : j + width],
                ROWS_BY_COLUMNS,
                preferred_element_type=F32,
            )
            total = grad_e * grad_e if total is None else total + grad_e * grad_e
        out_ref[:, j : j + width] = total * (1.0 / (EXAMPLES * SEQ))


def gathered(hidden_act, out_grad, down_weight):
    grad = lax.all_gather(out_grad, "row", axis=0, tiled=True)
    act = lax.all_gather(hidden_act, "col", axis=0, tiled=True)
    part = lax.dot_general(grad, down_weight, ROWS_BY_ROWS, preferred_element_type=F32)
    summed = lax.psum_scatter(part, "col", scatter_dimension=0, tiled=True)
    tokens, rows = act.shape
    columns = grad.shape[1]
    block = largest_block(rows, 256)
    fisher = pl.pallas_call(
        functools.partial(whole_kernel, width=largest_block(columns, 256)),
        out_shape=jax.ShapeDtypeStruct((rows, columns), F32),
        grid=(rows // block,),
        in_specs=[
            pl.BlockSpec((tokens, block), lambda i: (0, i)),
            pl.BlockSpec((tokens, columns), lambda i: (0, 0), pipeline_mode=pl.Buffered(1)),
        ],
        out_specs=pl.BlockSpec((block, columns), lambda i: (i, 0)),
        scratch_shapes=[pltpu.VMEM((EXAMPLES, block, LANES), act.dtype)],
        compiler_params=params(),
        name="fisher",
    )(act, grad)
    return fisher, summed.astype(jnp.bfloat16)


def solution(mesh):
    row_size, col_size = mesh.shape["row"], mesh.shape["col"]
    placed = (P("col", "row"), P("row", "col"), P("row", "col"))

    def on_mesh(per_device):
        return jax.shard_map(
            per_device,
            mesh=mesh,
            in_specs=placed,
            out_specs=(P("row", "col"), P("col", "row")),
            check_vma=False,
        )

    def per_device(hidden_act, out_grad, down_weight):
        return pipelined(hidden_act, out_grad, down_weight, row_size, col_size)

    if row_size != EXAMPLES or col_size != 4:
        return on_mesh(gathered)
    return on_mesh(per_device)
```

time: 246 us -> 193 us (0.78)
  waiting for transfers between devices: 135 us -> 47.2 us
  Pallas kernels: 65.1 us -> 122 us
  matrix products: 29.3 us -> 0 us
  starting transfers between devices: 0.11 us -> 20.6 us
  between operations: 13.7 us -> 0.8 us
    all_gather x2 -> x0, waiting for transfers between devices: 113 us -> none  [the longest x1 103 us: per_device(): grad_whole = lax.all_gather(out_grad, 'row', axis=0, tiled=True)]
    pallas_call x1 -> x12, Pallas kernels: 65.1 us -> 122 us  [the longest x6 76.2 us: fisher_part(): pl.pallas_call(functools.partial(fisher_kernel, width=largest_block(part,...]
    ppermute x0 -> x20, waiting for transfers between devices: none -> 47.2 us  [the longest x8 30.9 us: ring_gather(): from_left = lax.ppermute(from_left, 'row', right)]
    dot_general x1 -> x0, matrix products: 29.3 us -> none  [per_device(): lax.dot_general(grad_whole, down_weight, (((1,), (1,)), ((), ())), prefer...]
    ppermute x0 -> x20, starting transfers between devices: none -> 20.6 us  [the longest x8 13.2 us: ring_gather(): from_left = lax.ppermute(from_left, 'row', right)]
    reduce_scatter x1 -> x0, waiting for transfers between devices: 20.3 us -> none  [per_device(): lax.psum_scatter(lax.dot_general(grad_whole, down_weight, (((1,), (1,)),...]
  transfers between devices with their start and end apart: 3 -> 20, of which waited for: 3 -> 8; matrix products, arithmetic and copies ran while one was open for 12% -> 1% of each run, Pallas kernels for 26% -> 61%
where the time goes in v2:
time: 193 us
  Pallas kernels  122 us (63%)
  waiting for transfers between devices  47.2 us (24%)
  starting transfers between devices  20.6 us (11%)
  local copies, waits for them, and re-layouts  2.05 us (1%)
    pallas_call x6, Pallas kernels, fisher_part(): pl.pallas_call(functools.partial(fisher_kernel, width=largest_block(part,...  76.2 us
    pallas_call x2, Pallas kernels, hidden_part(): pl.pallas_call(functools.partial(hidden_kernel, places=places, block=bloc...  34.9 us
    ppermute x8, waiting for transfers between devices, ring_gather(): from_left = lax.ppermute(from_left, 'row', right)  30.9 us
    ppermute x6, waiting for transfers between devices, ring_gather(): from_right = lax.ppermute(from_right, 'row', left)  16.3 us
    ppermute x8, starting transfers between devices, ring_gather(): from_left = lax.ppermute(from_left, 'row', right)  13.2 us
    pallas_call x2, Pallas kernels, by_rows(): pl.pallas_call(kernel, out_shape=jax.ShapeDtypeStruct((rows, out_columns)...  6.12 us
    pallas_call x2, Pallas kernels, turned(): pl.pallas_call(functools.partial(turn_kernel, slot=slot, step=largest_blo...  4.53 us
  transfers between devices with their start and end apart: 20, of which 8 were waited for; matrix products, arithmetic and copies ran while one was open for 1% of the time, Pallas kernels for 61%

profile of v2, /device:TPU:0, one launch (start us, length us, event | category | flops | bytes accessed | tf_op | source)
XLA Modules:
  0.0 193.1 jit_solution(10873566444588561094)
XLA Ops:
  0.6 1.1 slice.6.refs_0_
  1.7 3.1 %collective-permute-start.3 = (bf16[96,2560]{1,0:T(8,128)(2,1)S(1)}, bf16[96,2560]{1,0:T(8,128)(2,1)S(1)}, u32[]{:S(2)}, u32[]{:S(2)}) collective-permute-start(bf16[96,2560]{1,0:T(8,128)(2,1)S(1)} %slice.6.refs_0_), channel_id=1, source_target_pairs={{0,8},{8,16},{16,24},{24,28},{28,20},{20,12},{12,4},{4,0},{1,9},{9... | collective-permute-start | bytes 1474568 | tf_op jit(solution)/shard_map/ppermute | solution.py:266
  4.8 1.0 slice.7.refs_0_
  5.8 1.6 collective-permute-start.10
  7.4 1.5 collective-permute-start
  8.9 0.4 collective-permute-start.11
  9.4 12.9 %collective-permute-done.10.refs_1_ = bf16[96,1536]{1,0:T(8,128)(2,1)S(1)} collective-permute-done((bf16[96,1536]{1,0:T(8,128)(2,1)S(1)}, bf16[96,1536]{1,0:T(8,128)(2,1)S(1)}, u32[]{:S(2)}, u32[]{:S(2)}) %collective-permute-start.10) | collective-permute-done | bytes 294944 | tf_op jit(solution)/shard_map/ppermute | solution.py:266
  22.3 1.8 collective-permute-start.12
  24.1 0.2 collective-permute-start.4
  24.3 0.0 collective-permute-done.3.refs_1_
  24.3 1.8 collective-permute-start.5
  26.1 0.0 collective-permute-done.11.refs_2_
  26.1 0.2 collective-permute-start.13
  26.3 5.8 %collective-permute-done.12.refs_3_ = bf16[96,1536]{1,0:T(8,128)(2,1)S(1)} collective-permute-done((bf16[96,1536]{1,0:T(8,128)(2,1)S(1)}, bf16[96,1536]{1,0:T(8,128)(2,1)S(1)}, u32[]{:S(2)}, u32[]{:S(2)}) %collective-permute-start.12) | collective-permute-done | bytes 294944 | tf_op jit(solution)/shard_map/ppermute | solution.py:266
  32.2 1.8 collective-permute-start.14
  34.0 8.4 %collective-permute-done.13.refs_4_ = bf16[96,1536]{1,0:T(8,128)(2,1)S(1)} collective-permute-done((bf16[96,1536]{1,0:T(8,128)(2,1)S(1)}, bf16[96,1536]{1,0:T(8,128)(2,1)S(1)}, u32[]{:S(2)}, u32[]{:S(2)}) %collective-permute-start.13) | collective-permute-done | bytes 294944 | tf_op jit(solution)/shard_map/ppermute | solution.py:269
  42.3 0.5 collective-permute-start.15
  42.8 0.0 collective-permute-done.4.refs_2_
  42.8 0.0 collective-permute-start.2
  42.9 4.6 %collective-permute-done.14.refs_5_ = bf16[96,1536]{1,0:T(8,128)(2,1)S(1)} collective-permute-done((bf16[96,1536]{1,0:T(8,128)(2,1)S(1)}, bf16[96,1536]{1,0:T(8,128)(2,1)S(1)}, u32[]{:S(2)}, u32[]{:S(2)}) %collective-permute-start.14) | collective-permute-done | bytes 294944 | tf_op jit(solution)/shard_map/ppermute | solution.py:266
  47.4 1.5 collective-permute-start.6
  48.9 0.0 collective-permute-done.5.refs_3_
  48.9 0.6 collective-permute-start.7
  49.4 0.4 collective-permute-done.15.refs_6_
  49.9 1.9 collective-permute-start.16
  51.8 0.7 add_convert_fusion
  52.5 7.5 %collective-permute-done.6.refs_4_ = bf16[96,2560]{1,0:T(8,128)(2,1)} collective-permute-done((bf16[96,2560]{1,0:T(8,128)(2,1)}, bf16[96,2560]{1,0:T(8,128)(2,1)}, u32[]{:S(2)}, u32[]{:S(2)}) %collective-permute-start.6) | collective-permute-done | bytes 491552 | tf_op jit(solution)/shard_map/ppermute | solution.py:269
  59.9 0.8 collective-permute-start.8
  60.7 0.0 collective-permute-done.refs_0_
  60.7 0.0 collective-permute-start.1
  60.7 2.6 %collective-permute-done.7.refs_5_ = bf16[96,2560]{1,0:T(8,128)(2,1)} collective-permute-done((bf16[96,2560]{1,0:T(8,128)(2,1)}, bf16[96,2560]{1,0:T(8,128)(2,1)}, u32[]{:S(2)}, u32[]{:S(2)}) %collective-permute-start.7) | collective-permute-done | bytes 491552 | tf_op jit(solution)/shard_map/ppermute | solution.py:266
  63.3 0.6 collective-permute-start.9
  63.9 5.1 %collective-permute-done.16.refs_7_ = bf16[96,1536]{1,0:T(8,128)(2,1)S(1)} collective-permute-done((bf16[96,1536]{1,0:T(8,128)(2,1)S(1)}, bf16[96,1536]{1,0:T(8,128)(2,1)S(1)}, u32[]{:S(2)}, u32[]{:S(2)}) %collective-permute-start.16) | collective-permute-done | bytes 294944 | tf_op jit(solution)/shard_map/ppermute | solution.py:266
  68.9 0.0 copy-start
  68.9 13.8 %shard_map.67 = (f32[192,3328]{1,0:T(8,128)S(1)}, f32[192,3328]{1,0:T(8,128)S(1)}, f32[192,3328]{1,0:T(8,128)}, f32[192,3328]{1,0:T(8,128)S(1)}) custom-call(s32[8]{0:T(128)S(1)} %get-tuple-element.20.to_ref, bf16[96,1536]{1,0:T(8,128)(2,1)S(1)} %slice.7.refs_0_, bf16[96,1536]{1,0:T(8,128)(2,1)S(1)} %collective-permute-done.10.refs_1_, ...), custom_call_target="tpu_custom_call" | custom-call | flops 7851737088 | bytes 10223616 | tf_op jit(solution)/shard_map/pallas_call | solution.py:191
  82.8 0.0 collective-permute-done.2.refs_1_
  82.8 0.0 copy-done
  82.8 2.3 %shard_map.59.refs_2_ = bf16[8,3328,128]{2,1,0:T(8,128)(2,1)S(1)} custom-call(bf16[192,3328]{1,0:T(8,128)(2,1)S(1)} %copy-done, bf16[192,3328]{1,0:T(8,128)(2,1)} %collective-permute-done.2.refs_1_), custom_call_target="tpu_custom_call" | custom-call | flops 2555904 | bytes 5111808 | tf_op jit(solution)/shard_map/pallas_call | solution.py:51
  85.0 0.0 collective-permute-done.8.refs_6_
  85.1 0.0 collective-permute-done.9.refs_7_
  85.1 21.1 %shard_map.68 = (f32[192,3328]{1,0:T(8,128)S(1)}, f32[192,3328]{1,0:T(8,128)S(1)}, f32[192,3328]{1,0:T(8,128)}, f32[192,3328]{1,0:T(8,128)S(1)}) custom-call(s32[8]{0:T(128)S(1)} %get-tuple-element.20.to_ref, bf16[96,2560]{1,0:T(8,128)(2,1)S(1)} %slice.6.refs_0_, ...), custom_call_target="tpu_custom_call", output_to_operand_aliasing={{0}: (10, {}), {1}: (11, {}), {2}: (12, {}), {3}: (13, {})} | custom-call | flops 13086228480 | bytes 17039360 | tf_op jit(solution)/shard_map/pallas_call | solution.py:191
  106.1 0.1 collective-permute-start.17
  106.2 0.5 collective-permute-start.18
  106.7 0.0 collective-permute-done.1.refs_1_
  106.7 2.3 %shard_map.60.rows_ref = bf16[8,3328,128]{2,1,0:T(8,128)(2,1)S(1)} custom-call(bf16[192,3328]{1,0:T(8,128)(2,1)} %collective-permute-done.refs_0_, bf16[192,3328]{1,0:T(8,128)(2,1)S(1)} %collective-permute-done.1.refs_1_, bf16[8,3328,128]{2,1,0:T(8,128)(2,1)S(1)} %shard_map.59.refs_2_), custom_call_target="tpu_custom_call", output_to_operand_aliasing={{}: (2, {})} | custom-call | flops 2555904 | bytes 5111808 | tf_op jit(solution)/shard_map/pallas_call | solution.py:51
  109.0 7.6 %shard_map.61.refs_8_ = f32[3328,4096]{1,0:T(8,128)} custom-call(s32[8]{0:T(128)S(1)} %get-tuple-element.21.at_ref, bf16[8,3328,128]{2,1,0:T(8,128)(2,1)S(1)} %shard_map.60.rows_ref, bf16[96,1536]{1,0:T(8,128)(2,1)S(1)} %slice.7.refs_0_, bf16[96,1536]{1,0:T(8,128)(2,1)S(1)} %collective-permute-done.10.refs_1_, ...), custom_call_target="tpu_custom_call" | custom-call | flops 4907335680 | bytes 5111808 | tf_op jit(solution)/shard_map/pallas_call | solution.py:119
  116.6 10.6 %shard_map.62.refs_8_ = f32[3328,4096]{1,0:T(8,128)} custom-call(s32[8]{0:T(128)S(1)} %get-tuple-element.21.at_ref, bf16[8,3328,128]{2,1,0:T(8,128)(2,1)S(1)} %shard_map.60.rows_ref, bf16[96,1536]{1,0:T(8,128)(2,1)S(1)} %slice.7.refs_0_, bf16[96,1536]{1,0:T(8,128)(2,1)S(1)} %collective-permute-done.10.refs_1_, ...), custom_call_target="tpu_custom_call", output_to_operand_aliasing={{}: (10, {})} | custom-call | flops 7361003520 | bytes 7667712 | tf_op jit(solution)/shard_map/pallas_call | solution.py:119
  127.2 10.6 %shard_map.63.refs_8_ = f32[3328,4096]{1,0:T(8,128)} custom-call(s32[8]{0:T(128)S(1)} %get-tuple-element.21.at_ref, bf16[8,3328,128]{2,1,0:T(8,128)(2,1)S(1)} %shard_map.60.rows_ref, bf16[96,1536]{1,0:T(8,128)(2,1)S(1)} %slice.7.refs_0_, bf16[96,1536]{1,0:T(8,128)(2,1)S(1)} %collective-permute-done.10.refs_1_, ...), custom_call_target="tpu_custom_call", output_to_operand_aliasing={{}: (10, {})} | custom-call | flops 7361003520 | bytes 7667712 | tf_op jit(solution)/shard_map/pallas_call | solution.py:119
  137.9 12.6 %shard_map.64.refs_8_ = f32[3328,4096]{1,0:T(8,128)} custom-call(s32[8]{0:T(128)S(1)} %get-tuple-element.21.at_ref, bf16[8,3328,128]{2,1,0:T(8,128)(2,1)S(1)} %shard_map.60.rows_ref, bf16[96,2560]{1,0:T(8,128)(2,1)S(1)} %slice.6.refs_0_, bf16[96,2560]{1,0:T(8,128)(2,1)S(1)} %collective-permute-done.3.refs_1_, ...), custom_call_target="tpu_custom_call", output_to_operand_aliasing={{}: (10, {})} | custom-call | flops 8178892800 | bytes 8519680 | tf_op jit(solution)/shard_map/pallas_call | solution.py:119
  150.5 0.0 collective-permute-done.18.b_ref
  150.5 1.4 shard_map.69
  151.9 1.7 collective-permute-start.19
  153.6 17.2 %shard_map.65.refs_8_ = f32[3328,4096]{1,0:T(8,128)} custom-call(s32[8]{0:T(128)S(1)} %get-tuple-element.21.at_ref, bf16[8,3328,128]{2,1,0:T(8,128)(2,1)S(1)} %shard_map.60.rows_ref, bf16[96,2560]{1,0:T(8,128)(2,1)S(1)} %slice.6.refs_0_, bf16[96,2560]{1,0:T(8,128)(2,1)S(1)} %collective-permute-done.3.refs_1_, ...), custom_call_target="tpu_custom_call", output_to_operand_aliasing={{}: (10, {})} | custom-call | flops 12268339200 | bytes 12779520 | tf_op jit(solution)/shard_map/pallas_call | solution.py:119
  170.9 17.5 %shard_map.66 = f32[3328,4096]{1,0:T(8,128)} custom-call(s32[8]{0:T(128)S(1)} %get-tuple-element.21.at_ref, bf16[8,3328,128]{2,1,0:T(8,128)(2,1)S(1)} %shard_map.60.rows_ref, bf16[96,2560]{1,0:T(8,128)(2,1)S(1)} %slice.6.refs_0_, bf16[96,2560]{1,0:T(8,128)(2,1)S(1)} %collective-permute-done.3.refs_1_, ...), custom_call_target="tpu_custom_call", output_to_operand_aliasing={{}: (10, {})} | custom-call | flops 12268339200 | bytes 12779520 | tf_op jit(solution)/shard_map/pallas_call | solution.py:119
  188.3 0.0 collective-permute-done.17.refs_1_
  188.4 0.0 collective-permute-done.19.refs_2_
  188.4 4.7 %shard_map.70 = bf16[192,3328]{1,0:T(8,128)(2,1)} custom-call(f32[192,3328]{1,0:T(8,128)S(1)} %get-tuple-element.16.refs_0_, f32[192,3328]{1,0:T(8,128)} %collective-permute-done.17.refs_1_, bf16[192,3456]{1,0:T(8,128)(2,1)S(1)} %collective-permute-done.19.refs_2_), custom_call_target="tpu_custom_call" | custom-call | flops 6389760 | bytes 5111808 | tf_op jit(solution)/shard_map/pallas_call | solution.py:243
Async XLA Ops:
  1.7 22.6 %collective-permute-start.3 = (bf16[96,2560]{1,0:T(8,128)(2,1)S(1)}, bf16[96,2560]{1,0:T(8,128)(2,1)S(1)}, u32[]{:S(2)}, u32[]{:S(2)}) collective-permute-start(bf16[96,2560]{1,0:T(8,128)(2,1)S(1)} %slice.6.refs_0_), channel_id=1, source_target_pairs={{0,8},{8,16},{16,24},{24,28},{28,20},{20,12},{12,4},{4,0},{1,9},{9... | collective-permute-start | bytes 1474568 | tf_op jit(solution)/shard_map/ppermute | solution.py:266
  5.8 16.5 %collective-permute-start.10 = (bf16[96,1536]{1,0:T(8,128)(2,1)S(1)}, bf16[96,1536]{1,0:T(8,128)(2,1)S(1)}, u32[]{:S(2)}, u32[]{:S(2)}) collective-permute-start(bf16[96,1536]{1,0:T(8,128)(2,1)S(1)} %slice.7.refs_0_), channel_id=1, source_target_pairs={{0,8},{8,16},{16,24},{24,28},{28,20},{20,12},{12,4},{4,0},{1,9},{9... | collective-permute-start | bytes 884744 | tf_op jit(solution)/shard_map/ppermute | solution.py:266
  7.4 53.3 %collective-permute-start = (bf16[192,3328]{1,0:T(8,128)(2,1)}, bf16[192,3328]{1,0:T(8,128)(2,1)}, u32[]{:S(2)}, u32[]{:S(2)}) collective-permute-start(bf16[192,3328]{1,0:T(8,128)(2,1)} %refs_0_.1), channel_id=1, source_target_pairs={{0,2},{1,3},{2,0},{3,1},{4,6},{5,7},{6,4},{7,5},{8,10},{9,11},{10,... | collective-permute-start | bytes 3833864 | tf_op jit(solution)/shard_map/ppermute | solution.py:299
  8.9 17.2 %collective-permute-start.11 = (bf16[96,1536]{1,0:T(8,128)(2,1)S(1)}, bf16[96,1536]{1,0:T(8,128)(2,1)S(1)}, u32[]{:S(2)}, u32[]{:S(2)}) collective-permute-start(bf16[96,1536]{1,0:T(8,128)(2,1)S(1)} %slice.7.refs_0_), channel_id=1, source_target_pairs={{8,0},{16,8},{24,16},{28,24},{20,28},{12,20},{4,12},{0,4},{9,1},{1... | collective-permute-start | bytes 884744 | tf_op jit(solution)/shard_map/ppermute | solution.py:269
  22.3 9.9 %collective-permute-start.12 = (bf16[96,1536]{1,0:T(8,128)(2,1)S(1)}, bf16[96,1536]{1,0:T(8,128)(2,1)S(1)}, u32[]{:S(2)}, u32[]{:S(2)}) collective-permute-start(bf16[96,1536]{1,0:T(8,128)(2,1)S(1)} %collective-permute-done.10.refs_1_), channel_id=1, source_target_pairs={{0,8},{8,16},{16,24},{24,28},{28,20},{20,12},{12,4},{4,0},{1,9},{9... | collective-permute-start | bytes 884744 | tf_op jit(solution)/shard_map/ppermute | solution.py:266
  24.1 18.8 %collective-permute-start.4 = (bf16[96,2560]{1,0:T(8,128)(2,1)S(1)}, bf16[96,2560]{1,0:T(8,128)(2,1)}, u32[]{:S(2)}, u32[]{:S(2)}) collective-permute-start(bf16[96,2560]{1,0:T(8,128)(2,1)S(1)} %slice.6.refs_0_), channel_id=1, source_target_pairs={{8,0},{16,8},{24,16},{28,24},{20,28},{12,20},{4,12},{0,4},{9,1},{1... | collective-permute-start | bytes 1474568 | tf_op jit(solution)/shard_map/ppermute | solution.py:269
  24.3 24.6 %collective-permute-start.5 = (bf16[96,2560]{1,0:T(8,128)(2,1)S(1)}, bf16[96,2560]{1,0:T(8,128)(2,1)}, u32[]{:S(2)}, u32[]{:S(2)}) collective-permute-start(bf16[96,2560]{1,0:T(8,128)(2,1)S(1)} %collective-permute-done.3.refs_1_), channel_id=1, source_target_pairs={{0,8},{8,16},{16,24},{24,28},{28,20},{20,12},{12,4},{4,0},{1,9},{9... | collective-permute-start | bytes 1474568 | tf_op jit(solution)/shard_map/ppermute | solution.py:266
  26.1 16.2 %collective-permute-start.13 = (bf16[96,1536]{1,0:T(8,128)(2,1)S(1)}, bf16[96,1536]{1,0:T(8,128)(2,1)S(1)}, u32[]{:S(2)}, u32[]{:S(2)}) collective-permute-start(bf16[96,1536]{1,0:T(8,128)(2,1)S(1)} %collective-permute-done.11.refs_2_), channel_id=1, source_target_pairs={{8,0},{16,8},{24,16},{28,24},{20,28},{12,20},{4,12},{0,4},{9,1},{1... | collective-permute-start | bytes 884744 | tf_op jit(solution)/shard_map/ppermute | solution.py:269
  32.2 15.3 %collective-permute-start.14 = (bf16[96,1536]{1,0:T(8,128)(2,1)S(1)}, bf16[96,1536]{1,0:T(8,128)(2,1)S(1)}, u32[]{:S(2)}, u32[]{:S(2)}) collective-permute-start(bf16[96,1536]{1,0:T(8,128)(2,1)S(1)} %collective-permute-done.12.refs_3_), channel_id=1, source_target_pairs={{0,8},{8,16},{16,24},{24,28},{28,20},{20,12},{12,4},{4,0},{1,9},{9... | collective-permute-start | bytes 884744 | tf_op jit(solution)/shard_map/ppermute | solution.py:266
  42.3 7.5 %collective-permute-start.15 = (bf16[96,1536]{1,0:T(8,128)(2,1)S(1)}, bf16[96,1536]{1,0:T(8,128)(2,1)S(1)}, u32[]{:S(2)}, u32[]{:S(2)}) collective-permute-start(bf16[96,1536]{1,0:T(8,128)(2,1)S(1)} %collective-permute-done.13.refs_4_), channel_id=1, source_target_pairs={{8,0},{16,8},{24,16},{28,24},{20,28},{12,20},{4,12},{0,4},{9,1},{1... | collective-permute-start | bytes 884744 | tf_op jit(solution)/shard_map/ppermute | solution.py:269
  42.8 39.9 %collective-permute-start.2 = (bf16[192,3328]{1,0:T(8,128)(2,1)}, bf16[192,3328]{1,0:T(8,128)(2,1)}, u32[]{:S(2)}, u32[]{:S(2)}) collective-permute-start(bf16[192,3328]{1,0:T(8,128)(2,1)} %refs_0_.1), channel_id=1, source_target_pairs={{0,1},{1,0},{2,3},{3,2},{4,5},{5,4},{6,7},{7,6},{8,9},{9,8},{10,11... | collective-permute-start | bytes 3833864 | tf_op jit(solution)/shard_map/ppermute | solution.py:300
  47.4 12.5 %collective-permute-start.6 = (bf16[96,2560]{1,0:T(8,128)(2,1)}, bf16[96,2560]{1,0:T(8,128)(2,1)}, u32[]{:S(2)}, u32[]{:S(2)}) collective-permute-start(bf16[96,2560]{1,0:T(8,128)(2,1)} %collective-permute-done.4.refs_2_), channel_id=1, source_target_pairs={{8,0},{16,8},{24,16},{28,24},{20,28},{12,20},{4,12},{0,4},{9,1},{1... | collective-permute-start | bytes 1474568 | tf_op jit(solution)/shard_map/ppermute | solution.py:269
  48.9 14.4 %collective-permute-start.7 = (bf16[96,2560]{1,0:T(8,128)(2,1)}, bf16[96,2560]{1,0:T(8,128)(2,1)}, u32[]{:S(2)}, u32[]{:S(2)}) collective-permute-start(bf16[96,2560]{1,0:T(8,128)(2,1)} %collective-permute-done.5.refs_3_), channel_id=1, source_target_pairs={{0,8},{8,16},{16,24},{24,28},{28,20},{20,12},{12,4},{4,0},{1,9},{9... | collective-permute-start | bytes 1474568 | tf_op jit(solution)/shard_map/ppermute | solution.py:266
  49.9 19.0 %collective-permute-start.16 = (bf16[96,1536]{1,0:T(8,128)(2,1)S(1)}, bf16[96,1536]{1,0:T(8,128)(2,1)S(1)}, u32[]{:S(2)}, u32[]{:S(2)}) collective-permute-start(bf16[96,1536]{1,0:T(8,128)(2,1)S(1)} %collective-permute-done.14.refs_5_), channel_id=1, source_target_pairs={{0,8},{8,16},{16,24},{24,28},{28,20},{20,12},{12,4},{4,0},{1,9},{9... | collective-permute-start | bytes 884744 | tf_op jit(solution)/shard_map/ppermute | solution.py:266
  59.9 25.1 %collective-permute-start.8 = (bf16[96,2560]{1,0:T(8,128)(2,1)}, bf16[96,2560]{1,0:T(8,128)(2,1)S(1)}, u32[]{:S(2)}, u32[]{:S(2)}) collective-permute-start(bf16[96,2560]{1,0:T(8,128)(2,1)} %collective-permute-done.6.refs_4_), channel_id=1, source_target_pairs={{8,0},{16,8},{24,16},{28,24},{20,28},{12,20},{4,12},{0,4},{9,1},{1... | collective-permute-start | bytes 1474568 | tf_op jit(solution)/shard_map/ppermute | solution.py:269
  60.7 46.0 %collective-permute-start.1 = (bf16[192,3328]{1,0:T(8,128)(2,1)}, bf16[192,3328]{1,0:T(8,128)(2,1)S(1)}, u32[]{:S(2)}, u32[]{:S(2)}) collective-permute-start(bf16[192,3328]{1,0:T(8,128)(2,1)} %collective-permute-done.refs_0_), channel_id=1, source_target_pairs={{0,1},{1,0},{2,3},{3,2},{4,5},{5,4},{6,7},{7,6},{8,9},{9,8},{10,11... | collective-permute-start | bytes 3833864 | tf_op jit(solution)/shard_map/ppermute | solution.py:300
  63.3 21.8 %collective-permute-start.9 = (bf16[96,2560]{1,0:T(8,128)(2,1)}, bf16[96,2560]{1,0:T(8,128)(2,1)S(1)}, u32[]{:S(2)}, u32[]{:S(2)}) collective-permute-start(bf16[96,2560]{1,0:T(8,128)(2,1)} %collective-permute-done.7.refs_5_), channel_id=1, source_target_pairs={{0,8},{8,16},{16,24},{24,28},{28,20},{20,12},{12,4},{4,0},{1,9},{9... | collective-permute-start | bytes 1474568 | tf_op jit(solution)/shard_map/ppermute | solution.py:266
  68.9 13.8 %copy-start = (bf16[192,3328]{1,0:T(8,128)(2,1)S(1)}, bf16[192,3328]{1,0:T(8,128)(2,1)}, u32[]{:S(2)}) copy-start(bf16[192,3328]{1,0:T(8,128)(2,1)} %refs_0_.1) | copy-start | bytes 3833860
  106.1 82.2 %collective-permute-start.17 = (f32[192,3328]{1,0:T(8,128)}, f32[192,3328]{1,0:T(8,128)}, u32[]{:S(2)}, u32[]{:S(2)}) collective-permute-start(f32[192,3328]{1,0:T(8,128)} %get-tuple-element.17), channel_id=1, source_target_pairs={{0,1},{1,0},{2,3},{3,2},{4,5},{5,4},{6,7},{7,6},{8,9},{9,8},{10,11... | collective-permute-start | bytes 7667720 | tf_op jit(solution)/shard_map/ppermute | solution.py:330
  106.2 44.3 %collective-permute-start.18 = (f32[192,3328]{1,0:T(8,128)S(1)}, f32[192,3328]{1,0:T(8,128)S(1)}, u32[]{:S(2)}, u32[]{:S(2)}) collective-permute-start(f32[192,3328]{1,0:T(8,128)S(1)} %get-tuple-element.19), channel_id=1, source_target_pairs={{0,1},{1,0},{2,3},{3,2},{4,5},{5,4},{6,7},{7,6},{8,9},{9,8},{10,11... | collective-permute-start | bytes 7667720 | tf_op jit(solution)/shard_map/ppermute | solution.py:327
  151.9 36.4 %collective-permute-start.19 = (bf16[192,3456]{1,0:T(8,128)(2,1)S(1)}, bf16[192,3456]{1,0:T(8,128)(2,1)S(1)}, u32[]{:S(2)}, u32[]{:S(2)}) collective-permute-start(bf16[192,3456]{1,0:T(8,128)(2,1)S(1)} %shard_map.69), channel_id=1, source_target_pairs={{0,2},{1,3},{2,0},{3,1},{4,6},{5,7},{6,4},{7,5},{8,10},{9,11},{10,... | collective-permute-start | bytes 3981320 | tf_op jit(solution)/shard_map/ppermute | solution.py:329

commit v3 on v2

--- a/solution.py
+++ b/solution.py
@@ -13,8 +13,10 @@
 EXAMPLES = 8
 LANES = 128
 EIGHTHS = (3, 5)
-SPLITS = 3
-BUFFERS = 4
+CUTS = ((0, 2, 5, 8), (0, 2, 8))
+BUFFERS = 3
+GROUP = 16
+HALVED = 1
 POWER_TOP = 2.0**7.75
 
 F32 = jnp.float32
@@ -61,8 +63,15 @@
     )(*acts, *held)
 
 
-def fisher_kernel(at_ref, rows_ref, *refs, width, part, block, first, blocks, start):
-    grad_refs = refs[:EXAMPLES]
+def columns_of(refs, slot, start, width):
+    if slot < EXAMPLES - 1:
+        return refs[slot].at[:, start : start + width]
+    held = refs[-1].shape[1]
+    return refs[slot + start // held].at[:, start % held : start % held + width]
+
+
+def fisher_kernel(at_ref, rows_ref, *refs, arrays, width, part, block, first, blocks, start):
+    grad_refs = refs[:arrays]
     fisher_ref, out_ref, sems = refs[-3:]
     parts = grad_refs[0].shape[1] // part
 
@@ -83,10 +92,10 @@
 
             for j in range(0, part, width):
                 total = None
-                for s, grad_ref in enumerate(grad_refs):
+                for s in range(EXAMPLES):
                     grad_e = lax.dot_general(
                         rows_ref[at_ref[s], units(i), :SEQ],
-                        grad_ref[:, n * part + j : n * part + j + width],
+                        columns_of(grad_refs, s, n * part + j, width)[...],
                         ROWS_BY_COLUMNS,
                         preferred_element_type=F32,
                     )
@@ -119,6 +128,7 @@
     return pl.pallas_call(
         functools.partial(
             fisher_kernel,
+            arrays=len(grads),
             width=largest_block(part, 256),
             part=part,
             block=block,
@@ -143,71 +153,88 @@
     )(*operands)
 
 
-def hidden_kernel(to_ref, *refs, places, block, start):
-    grad_refs, weight_ref = refs[:EXAMPLES], refs[EXAMPLES]
-    held_refs, out_refs = refs[EXAMPLES + 1 : -3 - places], refs[-3 - places : -3]
-    tokens_ref, buffer_ref, sems = refs[-3:]
-    columns = grad_refs[0].shape[1]
-    blocks = weight_ref.shape[0] // block
+def hidden_kernel(to_ref, *refs, arrays, places, start):
+    grad_refs, weight_ref = refs[:arrays], refs[arrays]
+    held_refs, out_refs = refs[arrays + 1 : -5 - places], refs[-5 - places : -5]
+    tokens_ref, buffer_ref, tail_ref, sems, tail_sem = refs[-5:]
+    columns = tokens_ref.shape[2]
+    buffers, block = buffer_ref.shape[:2]
+    blocks, tail = weight_ref.shape[0] // block, weight_ref.shape[0] % block
 
     def units(i):
         return pl.ds(pl.multiple_of(i * block, block), block)
 
     def fetching(i):
-        slot = lax.rem(i, BUFFERS)
+        slot = lax.rem(i, buffers)
         return pltpu.make_async_copy(
             weight_ref.at[units(i), pl.ds(start, columns)], buffer_ref.at[slot], sems.at[slot]
         )
 
-    for i in range(min(BUFFERS - 1, blocks)):
+    last = pl.ds(blocks * block, tail)
+    fetching_tail = pltpu.make_async_copy(
+        weight_ref.at[last, pl.ds(start, columns)], tail_ref.at[pl.ds(0, tail)], tail_sem
+    )
+
+    for i in range(min(buffers - 1, blocks)):
         fetching(jnp.int32(i)).start()
+    if tail:
+        fetching_tail.start()
+    held = grad_refs[-1].shape[1]
     for s in range(EXAMPLES):
-        tokens_ref[to_ref[s]] = grad_refs[s][...]
-
-    def one_block(i, carry):
-        @pl.when(i + BUFFERS - 1 < blocks)
-        def _():
-            fetching(i + BUFFERS - 1).start()
-
-        fetching(i).wait()
+        for column in range(0, columns, held):
+            here = slice(column, column + held)
+            tokens_ref[to_ref[s], :, here] = columns_of(grad_refs, s, column, held)[...]
+
+    def multiplied(weights, here):
         tokens = tokens_ref[...].reshape(EXAMPLES * SEQ, columns)
-        part = lax.dot_general(
-            tokens, buffer_ref[lax.rem(i, BUFFERS)], ROWS_BY_ROWS, preferred_element_type=F32
-        )
+        part = lax.dot_general(tokens, weights, ROWS_BY_ROWS, preferred_element_type=F32)
         rows = part.shape[0] // places
         for n, out_ref in enumerate(out_refs):
             piece = part[n * rows : (n + 1) * rows]
-            out_ref[:, units(i)] = piece + held_refs[n][:, units(i)] if held_refs else piece
+            out_ref[:, here] = piece + held_refs[n][:, here] if held_refs else piece
+
+    def one_block(i, carry):
+        @pl.when(i + buffers - 1 < blocks)
+        def _():
+            fetching(i + buffers - 1).start()
+
+        fetching(i).wait()
+        multiplied(buffer_ref[lax.rem(i, buffers)], units(i))
         return carry
 
     lax.fori_loop(0, blocks, one_block, 0)
+    if tail:
+        fetching_tail.wait()
+        multiplied(tail_ref[:tail], last)
 
 
 def hidden_part(to, grads, weight, held, places, start):
     units = weight.shape[0]
     columns = grads[0].shape[1]
-    block = largest_block(units, 256)
+    block = 2 * largest_block(units, 256)
     rows = EXAMPLES * SEQ // places
     return pl.pallas_call(
-        functools.partial(hidden_kernel, places=places, block=block, start=start),
+        functools.partial(hidden_kernel, arrays=len(grads), places=places, start=start),
         out_shape=[jax.ShapeDtypeStruct((rows, units), F32)] * places,
         in_specs=[pl.BlockSpec(memory_space=pltpu.SMEM)]
-        + [in_vmem()] * EXAMPLES
+        + [in_vmem()] * len(grads)
         + [pl.BlockSpec(memory_space=pl.ANY)]
         + [in_vmem()] * len(held),
         out_specs=[in_vmem()] * places,
         scratch_shapes=[
             pltpu.VMEM((EXAMPLES, SEQ, columns), weight.dtype),
             pltpu.VMEM((BUFFERS, block, columns), weight.dtype),
+            pltpu.VMEM((units % block or LANES, columns), weight.dtype),
             pltpu.SemaphoreType.DMA((BUFFERS,)),
+            pltpu.SemaphoreType.DMA(()),
         ],
-        input_output_aliases={2 + EXAMPLES + n: n for n in range(len(held))},
+        input_output_aliases={2 + len(grads) + n: n for n in range(len(held))},
         cost_estimate=pl.CostEstimate(
             flops=2 * EXAMPLES * SEQ * units * columns,
             bytes_accessed=2 * units * columns,
             transcendentals=0,
         ),
-        compiler_params=pltpu.CompilerParams(vmem_limit_bytes=28 << 20),
+        compiler_params=pltpu.CompilerParams(vmem_limit_bytes=22 << 20),
     )(to, *grads, weight, *held)
 
 
@@ -225,49 +252,89 @@
     code_ref[:, :units] = jnp.where(share < 0, -power, power).astype(code_ref.dtype)
 
 
-def decode_kernel(*refs):
-    mine_ref, other_ref, code_refs, out_ref = refs[0], refs[1], refs[2:-1], refs[-1]
-    total = mine_ref[...] + other_ref[...]
-    units = total.shape[1]
-    for code_ref in code_refs:
-        power = code_ref[:, :units].astype(F32)
-        root = jnp.exp(jnp.log(jnp.abs(power)) * (1.0 / 16))
-        scale = code_ref[:, units:].astype(F32)[:, :1] * (1.0 / POWER_TOP)
-        total = total + jnp.where(power < 0, -root, root) * scale
-    out_ref[...] = total.astype(out_ref.dtype)
-
-
-def by_rows(kernel, out_columns, dtype, *arrays):
-    rows = arrays[0].shape[0]
+def encoded(a, b):
+    rows, units = a.shape
     block = 48 if rows % 48 == 0 else rows
     return pl.pallas_call(
-        kernel,
-        out_shape=jax.ShapeDtypeStruct((rows, out_columns), dtype),
+        encode_kernel,
+        out_shape=jax.ShapeDtypeStruct((rows, units + LANES), jnp.bfloat16),
         grid=(rows // block,),
-        in_specs=[pl.BlockSpec((block, a.shape[1]), lambda i: (i, 0)) for a in arrays],
-        out_specs=pl.BlockSpec((block, out_columns), lambda i: (i, 0)),
+        in_specs=[pl.BlockSpec((block, units), lambda i: (i, 0))] * 2,
+        out_specs=pl.BlockSpec((block, units + LANES), lambda i: (i, 0)),
         cost_estimate=pl.CostEstimate(
-            flops=10 * rows * out_columns, bytes_accessed=8 * rows * out_columns, transcendentals=0
+            flops=10 * rows * units, bytes_accessed=10 * rows * units, transcendentals=0
         ),
         compiler_params=params(20),
-    )(*arrays)
+        name="encode",
+    )(a, b)
+
+
+def decode_kernel(*refs):
+    mine_ref, other_ref, code_refs = refs[0], refs[1], refs[2:-3]
+    result_ref, out_ref, sems = refs[-3:]
+    units = mine_ref.shape[1]
+    share = mine_ref.shape[0] // sems.shape[0]
+
+    def some_rows(i, carry):
+        rows = pl.ds(pl.multiple_of(i * GROUP, GROUP), GROUP)
+        total = mine_ref[rows, :] + other_ref[rows, :]
+        for code_ref in code_refs:
+            power = code_ref[rows, :units].astype(F32)
+            root = jnp.exp(jnp.log(jnp.abs(power)) * (1.0 / 16))
+            scale = code_ref[rows, units:].astype(F32)[:, :1] * (1.0 / POWER_TOP)
+            total = total + jnp.where(power < 0, -root, root) * scale
+        out_ref[rows, :] = total.astype(out_ref.dtype)
+        return carry
+
+    def sending(n):
+        rows = pl.ds(n * share, share)
+        return pltpu.make_async_copy(out_ref.at[rows], result_ref.at[rows], sems.at[n])
+
+    for n in range(sems.shape[0]):
+        lax.fori_loop(n * share // GROUP, (n + 1) * share // GROUP, some_rows, 0)
+        sending(n).start()
+    for n in range(sems.shape[0]):
+        sending(n).wait()
+
+
+def decoded(mine, other, codes):
+    rows, units = mine.shape
+    shares = 4 if rows % (4 * GROUP) == 0 else 1
+    return pl.pallas_call(
+        decode_kernel,
+        out_shape=jax.ShapeDtypeStruct((rows, units), jnp.bfloat16),
+        in_specs=[in_vmem()] * (2 + len(codes)),
+        out_specs=pl.BlockSpec(memory_space=pl.ANY),
+        scratch_shapes=[
+            pltpu.VMEM((rows, units), jnp.bfloat16),
+            pltpu.SemaphoreType.DMA((shares,)),
+        ],
+        cost_estimate=pl.CostEstimate(
+            flops=10 * rows * units, bytes_accessed=10 * rows * units, transcendentals=0
+        ),
+        compiler_params=pltpu.CompilerParams(vmem_limit_bytes=8 << 20),
+        name="decode",
+    )(mine, other, *codes)
 
 
 def ring_places(size):
     return list(range(0, size, 2)) + list(range(size - 1, 0, -2))
 
 
-def ring_gather(piece, size):
+def ring_gather(piece, size, halved):
     ring = ring_places(size)
     right = [(ring[n], ring[(n + 1) % size]) for n in range(size)]
     left = [(b, a) for a, b in right]
     found, from_left, from_right = [piece], piece, piece
-    for step in range(1, size // 2 + 1):
+    last, half = size // 2, piece.shape[1] // 2
+    for _ in range(1, last):
         from_left = lax.ppermute(from_left, "row", right)
-        found.append(from_left)
-        if step < size - size // 2:
-            from_right = lax.ppermute(from_right, "row", left)
-            found.append(from_right)
+        from_right = lax.ppermute(from_right, "row", left)
+        found += [from_left, from_right]
+    if not halved:
+        return found + [lax.ppermute(from_left, "row", right)]
+    found.append(lax.ppermute(from_left[:, :half], "row", right))
+    found.append(lax.ppermute(from_right[:, half:], "row", left))
     return found
 
 
@@ -300,7 +367,10 @@
         acts += [same, lax.ppermute(same, "col", other_core)]
 
     edges = [features * sum(EIGHTHS[:p]) // 8 for p in range(len(EIGHTHS) + 1)]
-    grads = [ring_gather(out_grad[:, a:b], row_size) for a, b in zip(edges, edges[1:])]
+    grads = [
+        ring_gather(out_grad[:, a:b], row_size, p < HALVED)
+        for p, (a, b) in enumerate(zip(edges, edges[1:]))
+    ]
 
     examples = ring_rows(row_size)
     col = lax.axis_index("col").astype(jnp.uint32)
@@ -316,19 +386,19 @@
         rows = (turned(acts[2 * d : 2 * d + 2], rows, 2 * d * per_col),)
     shape = (units, features)
     blocks = units // row_block(units)
-    cuts = [blocks * n // SPLITS for n in range(SPLITS + 1)]
     fisher, sums = None, []
     for p, start in enumerate(edges[:-1]):
         sums = hidden_part(to, grads[p], down_weight, sums, 2 * chips, start)
+        cuts = [blocks * eighths // 8 for eighths in CUTS[p]]
         for a, b in zip(cuts, cuts[1:]):
             fisher = fisher_part(at, rows[0], grads[p], fisher, shape, a, b - a, start)
     codes = []
     for d in range(1, chips):
         given = lax.ppermute(sums[2 * d - 2], "col", other_core)
-        code = by_rows(encode_kernel, units + LANES, jnp.bfloat16, sums[2 * d - 1], given)
+        code = encoded(sums[2 * d - 1], given)
         codes.append(lax.ppermute(code, "col", ahead[d]))
     given = lax.ppermute(sums[-2], "col", other_core)
-    return fisher, by_rows(decode_kernel, units, jnp.bfloat16, sums[-1], given, *codes)
+    return fisher, decoded(sums[-1], given, codes)
 
 
 def whole_kernel(act_ref, grad_ref, out_ref, rows_ref, *, width):

time: 193 us -> 184 us (0.953)
  Pallas kernels: 122 us -> 116 us
  waiting for transfers between devices: 47.2 us -> 42.9 us
    ppermute x6, waiting for transfers between devices: 16.3 us -> 9.14 us  [ring_gather(): from_right = lax.ppermute(from_right, 'row', left)]
    ppermute x0 -> x3, waiting for transfers between devices: none -> 5.72 us  [the longest x1 5.71 us: ring_gather(): found.append(lax.ppermute(from_left[:, :half], 'row', right))]
    pallas_call x10 -> x9, Pallas kernels: 117 us -> 111 us  [the longest x5 72.9 us: fisher_part(): pl.pallas_call(functools.partial(fisher_kernel, arrays=len(grads), width=...]
    ppermute x8 -> x6, waiting for transfers between devices: 30.9 us -> 28 us  [ring_gather(): from_left = lax.ppermute(from_left, 'row', right)]
    ppermute x8 -> x6, starting transfers between devices: 13.2 us -> 10.5 us  [ring_gather(): from_left = lax.ppermute(from_left, 'row', right)]
    ppermute x0 -> x3, starting transfers between devices: none -> 2.58 us  [the longest x1 1.24 us: ring_gather(): found.append(lax.ppermute(from_left[:, :half], 'row', right))]
  transfers between devices with their start and end apart: 20 -> 21, of which waited for: 8 -> 7; matrix products, arithmetic and copies ran while one was open for 1% -> 1% of each run, Pallas kernels for 61% -> 61%
where the time goes in v3:
time: 184 us
  Pallas kernels  116 us (63%)
  waiting for transfers between devices  42.9 us (23%)
  starting transfers between devices  21.3 us (12%)
  local copies, waits for them, and re-layouts  2.07 us (1%)
    pallas_call x5, Pallas kernels, fisher_part(): pl.pallas_call(functools.partial(fisher_kernel, arrays=len(grads), width=...  72.9 us
    pallas_call x2, Pallas kernels, hidden_part(): pl.pallas_call(functools.partial(hidden_kernel, arrays=len(grads), places...  33.1 us
    ppermute x6, waiting for transfers between devices, ring_gather(): from_left = lax.ppermute(from_left, 'row', right)  28 us
    ppermute x6, starting transfers between devices, ring_gather(): from_left = lax.ppermute(from_left, 'row', right)  10.5 us
    ppermute x6, waiting for transfers between devices, ring_gather(): from_right = lax.ppermute(from_right, 'row', left)  9.14 us
    ppermute x1, waiting for transfers between devices, ring_gather(): found.append(lax.ppermute(from_left[:, :half], 'row', right))  5.71 us
    ppermute x6, starting transfers between devices, ring_gather(): from_right = lax.ppermute(from_right, 'row', left)  4.61 us
    pallas_call x2, Pallas kernels, turned(): pl.pallas_call(functools.partial(turn_kernel, slot=slot, step=largest_blo...  4.53 us
  transfers between devices with their start and end apart: 21, of which 7 were waited for; matrix products, arithmetic and copies ran while one was open for 1% of the time, Pallas kernels for 61%

profile of v3, /device:TPU:0, one launch (start us, length us, event | category | flops | bytes accessed | tf_op | source)
XLA Modules:
  0.0 183.9 jit_solution(2937027531324278818)
XLA Ops:
  0.6 1.1 slice.12.refs_0_
  1.7 3.1 %collective-permute-start.3 = (bf16[96,2560]{1,0:T(8,128)(2,1)S(1)}, bf16[96,2560]{1,0:T(8,128)(2,1)S(1)}, u32[]{:S(2)}, u32[]{:S(2)}) collective-permute-start(bf16[96,2560]{1,0:T(8,128)(2,1)S(1)} %slice.12.refs_0_), channel_id=1, source_target_pairs={{0,8},{8,16},{16,24},{24,28},{28,20},{20,12},{12,4},{4,0},{1,9},{9... | collective-permute-start | bytes 1474568 | tf_op jit(solution)/shard_map/ppermute | solution.py:331
  4.8 1.0 slice.13.refs_0_
  5.8 1.6 collective-permute-start.10
  7.4 1.5 collective-permute-start
  8.9 0.4 collective-permute-start.4
  9.4 0.4 collective-permute-start.11
  9.8 12.5 %collective-permute-done.10.refs_1_ = bf16[96,1536]{1,0:T(8,128)(2,1)S(1)} collective-permute-done((bf16[96,1536]{1,0:T(8,128)(2,1)S(1)}, bf16[96,1536]{1,0:T(8,128)(2,1)S(1)}, u32[]{:S(2)}, u32[]{:S(2)}) %collective-permute-start.10) | collective-permute-done | bytes 294944 | tf_op jit(solution)/shard_map/ppermute | solution.py:331
  22.3 1.8 collective-permute-start.12
  24.1 0.0 collective-permute-done.3.refs_1_
  24.1 1.6 collective-permute-start.5
  25.7 1.7 collective-permute-done.11.refs_2_
  27.3 0.4 collective-permute-start.13
  27.8 4.4 %collective-permute-done.12.refs_3_ = bf16[96,1536]{1,0:T(8,128)(2,1)S(1)} collective-permute-done((bf16[96,1536]{1,0:T(8,128)(2,1)S(1)}, bf16[96,1536]{1,0:T(8,128)(2,1)S(1)}, u32[]{:S(2)}, u32[]{:S(2)}) %collective-permute-start.12) | collective-permute-done | bytes 294944 | tf_op jit(solution)/shard_map/ppermute | solution.py:331
  32.2 1.8 collective-permute-start.14
  34.0 0.0 collective-permute-done.4.refs_2_
  34.0 0.2 collective-permute-start.6
  34.2 2.1 %collective-permute-done.13.refs_4_ = bf16[96,1536]{1,0:T(8,128)(2,1)S(1)} collective-permute-done((bf16[96,1536]{1,0:T(8,128)(2,1)S(1)}, bf16[96,1536]{1,0:T(8,128)(2,1)S(1)}, u32[]{:S(2)}, u32[]{:S(2)}) %collective-permute-start.13) | collective-permute-done | bytes 294944 | tf_op jit(solution)/shard_map/ppermute | solution.py:332
  36.3 0.0 collective-permute-start.2
  36.3 11.1 %collective-permute-done.14.refs_5_ = bf16[96,1536]{1,0:T(8,128)(2,1)S(1)} collective-permute-done((bf16[96,1536]{1,0:T(8,128)(2,1)S(1)}, bf16[96,1536]{1,0:T(8,128)(2,1)S(1)}, u32[]{:S(2)}, u32[]{:S(2)}) %collective-permute-start.14) | collective-permute-done | bytes 294944 | tf_op jit(solution)/shard_map/ppermute | solution.py:331
  47.4 1.5 collective-permute-start.15
  48.9 0.0 collective-permute-done.5.refs_3_
  48.9 0.6 collective-permute-start.7
  49.5 5.4 %collective-permute-done.15.refs_6_ = bf16[96,1536]{1,0:T(8,128)(2,1)S(1)} collective-permute-done((bf16[96,1536]{1,0:T(8,128)(2,1)S(1)}, bf16[96,1536]{1,0:T(8,128)(2,1)S(1)}, u32[]{:S(2)}, u32[]{:S(2)}) %collective-permute-start.15) | collective-permute-done | bytes 294944 | tf_op jit(solution)/shard_map/ppermute | solution.py:332
  54.8 1.2 collective-permute-start.16
  56.1 0.0 collective-permute-done.6.refs_4_
  56.1 0.8 collective-permute-start.17
  56.9 0.7 add_convert_fusion
  57.6 5.7 %collective-permute-done.16.refs_7_ = bf16[96,768]{1,0:T(8,128)(2,1)S(1)} collective-permute-done((bf16[96,768]{1,0:T(8,128)(2,1)S(1)}, bf16[96,768]{1,0:T(8,128)(2,1)S(1)}, u32[]{:S(2)}, u32[]{:S(2)}) %collective-permute-start.16) | collective-permute-done | bytes 147488 | tf_op jit(solution)/shard_map/ppermute | solution.py:336
  63.3 1.6 collective-permute-start.8
  64.9 0.0 collective-permute-done.refs_0_
  64.9 0.0 collective-permute-start.1
  64.9 0.0 collective-permute-done.7.refs_5_
  64.9 0.5 collective-permute-start.9
  65.4 0.0 collective-permute-done.17.refs_8_
  65.4 0.0 copy-start
  65.4 12.9 %shard_map.66 = (f32[192,3328]{1,0:T(8,128)S(1)}, f32[192,3328]{1,0:T(8,128)S(1)}, f32[192,3328]{1,0:T(8,128)}, f32[192,3328]{1,0:T(8,128)S(1)}) custom-call(s32[8]{0:T(128)S(1)} %get-tuple-element.20.to_ref, bf16[96,1536]{1,0:T(8,128)(2,1)S(1)} %slice.13.refs_0_, bf16[96,1536]{1,0:T(8,128)(2,1)S(1)} %collective-permute-done.10.refs_1_, ...), custom_call_target="tpu_custom_call" | custom-call | flops 7851737088 | bytes 10223616 | tf_op jit(solution)/shard_map/pallas_call | solution.py:216
  78.3 0.0 collective-permute-done.2.refs_1_
  78.3 0.0 copy-done
  78.3 2.3 %shard_map.59.refs_2_ = bf16[8,3328,128]{2,1,0:T(8,128)(2,1)S(1)} custom-call(bf16[192,3328]{1,0:T(8,128)(2,1)S(1)} %copy-done, bf16[192,3328]{1,0:T(8,128)(2,1)} %collective-permute-done.2.refs_1_), custom_call_target="tpu_custom_call" | custom-call | flops 2555904 | bytes 5111808 | tf_op jit(solution)/shard_map/pallas_call | solution.py:53
  80.6 0.0 collective-permute-done.8.refs_6_
  80.6 0.0 collective-permute-done.9.refs_7_
  80.6 20.2 %shard_map.67 = (f32[192,3328]{1,0:T(8,128)S(1)}, f32[192,3328]{1,0:T(8,128)S(1)}, f32[192,3328]{1,0:T(8,128)}, f32[192,3328]{1,0:T(8,128)S(1)}) custom-call(s32[8]{0:T(128)S(1)} %get-tuple-element.20.to_ref, bf16[96,2560]{1,0:T(8,128)(2,1)S(1)} %slice.12.refs_0_, ...), custom_call_target="tpu_custom_call", output_to_operand_aliasing={{0}: (10, {}), {1}: (11, {}), {2}: (12, {}), {3}: (13, {})} | custom-call | flops 13086228480 | bytes 17039360 | tf_op jit(solution)/shard_map/pallas_call | solution.py:216
  100.8 0.2 collective-permute-start.18
  101.0 0.3 collective-permute-start.19
  101.4 0.0 collective-permute-done.1.refs_1_
  101.4 2.3 %shard_map.60.rows_ref = bf16[8,3328,128]{2,1,0:T(8,128)(2,1)S(1)} custom-call(bf16[192,3328]{1,0:T(8,128)(2,1)} %collective-permute-done.refs_0_, bf16[192,3328]{1,0:T(8,128)(2,1)S(1)} %collective-permute-done.1.refs_1_, bf16[8,3328,128]{2,1,0:T(8,128)(2,1)S(1)} %shard_map.59.refs_2_), custom_call_target="tpu_custom_call", output_to_operand_aliasing={{}: (2, {})} | custom-call | flops 2555904 | bytes 5111808 | tf_op jit(solution)/shard_map/pallas_call | solution.py:53
  103.7 7.6 %shard_map.61.refs_9_ = f32[3328,4096]{1,0:T(8,128)} custom-call(s32[8]{0:T(128)S(1)} %get-tuple-element.21.at_ref, bf16[8,3328,128]{2,1,0:T(8,128)(2,1)S(1)} %shard_map.60.rows_ref, bf16[96,1536]{1,0:T(8,128)(2,1)S(1)} %slice.13.refs_0_, bf16[96,1536]{1,0:T(8,128)(2,1)S(1)} %collective-permute-done.10.refs_1_, ...), custom_call_target="tpu_custom_call" | custom-call | flops 4907335680 | bytes 5111808 | tf_op jit(solution)/shard_map/pallas_call | solution.py:128
  111.3 10.6 %shard_map.62.refs_9_ = f32[3328,4096]{1,0:T(8,128)} custom-call(s32[8]{0:T(128)S(1)} %get-tuple-element.21.at_ref, bf16[8,3328,128]{2,1,0:T(8,128)(2,1)S(1)} %shard_map.60.rows_ref, bf16[96,1536]{1,0:T(8,128)(2,1)S(1)} %slice.13.refs_0_, bf16[96,1536]{1,0:T(8,128)(2,1)S(1)} %collective-permute-done.10.refs_1_, ...), custom_call_target="tpu_custom_call", output_to_operand_aliasing={{}: (11, {})} | custom-call | flops 7361003520 | bytes 7667712 | tf_op jit(solution)/shard_map/pallas_call | solution.py:128
  121.9 10.8 %shard_map.63.refs_8_ = f32[3328,4096]{1,0:T(8,128)} custom-call(s32[8]{0:T(128)S(1)} %get-tuple-element.21.at_ref, bf16[8,3328,128]{2,1,0:T(8,128)(2,1)S(1)} %shard_map.60.rows_ref, bf16[96,1536]{1,0:T(8,128)(2,1)S(1)} %slice.13.refs_0_, bf16[96,1536]{1,0:T(8,128)(2,1)S(1)} %collective-permute-done.10.refs_1_, ...), custom_call_target="tpu_custom_call", output_to_operand_aliasing={{}: (11, {})} | custom-call | flops 7361003520 | bytes 7667712 | tf_op jit(solution)/shard_map/pallas_call | solution.py:128
  132.7 12.3 %shard_map.64.refs_8_ = f32[3328,4096]{1,0:T(8,128)} custom-call(s32[8]{0:T(128)S(1)} %get-tuple-element.21.at_ref, bf16[8,3328,128]{2,1,0:T(8,128)(2,1)S(1)} %shard_map.60.rows_ref, bf16[96,2560]{1,0:T(8,128)(2,1)S(1)} %slice.12.refs_0_, bf16[96,2560]{1,0:T(8,128)(2,1)S(1)} %collective-permute-done.3.refs_1_, ...), custom_call_target="tpu_custom_call", output_to_operand_aliasing={{}: (10, {})} | custom-call | flops 8178892800 | bytes 8519680 | tf_op jit(solution)/shard_map/pallas_call | solution.py:128
  144.9 0.0 collective-permute-done.19.b_ref
  145.0 1.4 encode.1
  146.4 1.6 collective-permute-start.20
  148.0 31.6 %shard_map.65 = f32[3328,4096]{1,0:T(8,128)} custom-call(s32[8]{0:T(128)S(1)} %get-tuple-element.21.at_ref, bf16[8,3328,128]{2,1,0:T(8,128)(2,1)S(1)} %shard_map.60.rows_ref, bf16[96,2560]{1,0:T(8,128)(2,1)S(1)} %slice.12.refs_0_, bf16[96,2560]{1,0:T(8,128)(2,1)S(1)} %collective-permute-done.3.refs_1_, ...), custom_call_target="tpu_custom_call", output_to_operand_aliasing={{}: (10, {})} | custom-call | flops 24536678400 | bytes 25559040 | tf_op jit(solution)/shard_map/pallas_call | solution.py:128
  179.6 0.0 collective-permute-done.18.refs_1_
  179.6 0.0 collective-permute-done.20.refs_2_
  179.6 4.2 %decode.1 = bf16[192,3328]{1,0:T(8,128)(2,1)} custom-call(f32[192,3328]{1,0:T(8,128)S(1)} %get-tuple-element.16.refs_0_, f32[192,3328]{1,0:T(8,128)} %collective-permute-done.18.refs_1_, bf16[192,3456]{1,0:T(8,128)(2,1)S(1)} %collective-permute-done.20.refs_2_), custom_call_target="tpu_custom_call" | custom-call | flops 6389760 | bytes 6389760 | tf_op jit(solution)/shard_map/decode/pallas_call | solution.py:303
  (2 shorter events, 0.0 us)
Async XLA Ops:
  1.7 22.4 %collective-permute-start.3 = (bf16[96,2560]{1,0:T(8,128)(2,1)S(1)}, bf16[96,2560]{1,0:T(8,128)(2,1)S(1)}, u32[]{:S(2)}, u32[]{:S(2)}) collective-permute-start(bf16[96,2560]{1,0:T(8,128)(2,1)S(1)} %slice.12.refs_0_), channel_id=1, source_target_pairs={{0,8},{8,16},{16,24},{24,28},{28,20},{20,12},{12,4},{4,0},{1,9},{9... | collective-permute-start | bytes 1474568 | tf_op jit(solution)/shard_map/ppermute | solution.py:331
  5.8 16.5 %collective-permute-start.10 = (bf16[96,1536]{1,0:T(8,128)(2,1)S(1)}, bf16[96,1536]{1,0:T(8,128)(2,1)S(1)}, u32[]{:S(2)}, u32[]{:S(2)}) collective-permute-start(bf16[96,1536]{1,0:T(8,128)(2,1)S(1)} %slice.13.refs_0_), channel_id=1, source_target_pairs={{0,8},{8,16},{16,24},{24,28},{28,20},{20,12},{12,4},{4,0},{1,9},{9... | collective-permute-start | bytes 884744 | tf_op jit(solution)/shard_map/ppermute | solution.py:331
  7.4 57.5 %collective-permute-start = (bf16[192,3328]{1,0:T(8,128)(2,1)}, bf16[192,3328]{1,0:T(8,128)(2,1)}, u32[]{:S(2)}, u32[]{:S(2)}) collective-permute-start(bf16[192,3328]{1,0:T(8,128)(2,1)} %refs_0_.1), channel_id=1, source_target_pairs={{0,2},{1,3},{2,0},{3,1},{4,6},{5,7},{6,4},{7,5},{8,10},{9,11},{10,... | collective-permute-start | bytes 3833864 | tf_op jit(solution)/shard_map/ppermute | solution.py:366
  8.9 25.1 %collective-permute-start.4 = (bf16[96,2560]{1,0:T(8,128)(2,1)S(1)}, bf16[96,2560]{1,0:T(8,128)(2,1)S(1)}, u32[]{:S(2)}, u32[]{:S(2)}) collective-permute-start(bf16[96,2560]{1,0:T(8,128)(2,1)S(1)} %slice.12.refs_0_), channel_id=1, source_target_pairs={{8,0},{16,8},{24,16},{28,24},{20,28},{12,20},{4,12},{0,4},{9,1},{1... | collective-permute-start | bytes 1474568 | tf_op jit(solution)/shard_map/ppermute | solution.py:332
  9.4 18.0 %collective-permute-start.11 = (bf16[96,1536]{1,0:T(8,128)(2,1)S(1)}, bf16[96,1536]{1,0:T(8,128)(2,1)S(1)}, u32[]{:S(2)}, u32[]{:S(2)}) collective-permute-start(bf16[96,1536]{1,0:T(8,128)(2,1)S(1)} %slice.13.refs_0_), channel_id=1, source_target_pairs={{8,0},{16,8},{24,16},{28,24},{20,28},{12,20},{4,12},{0,4},{9,1},{1... | collective-permute-start | bytes 884744 | tf_op jit(solution)/shard_map/ppermute | solution.py:332
  22.3 9.9 %collective-permute-start.12 = (bf16[96,1536]{1,0:T(8,128)(2,1)S(1)}, bf16[96,1536]{1,0:T(8,128)(2,1)S(1)}, u32[]{:S(2)}, u32[]{:S(2)}) collective-permute-start(bf16[96,1536]{1,0:T(8,128)(2,1)S(1)} %collective-permute-done.10.refs_1_), channel_id=1, source_target_pairs={{0,8},{8,16},{16,24},{24,28},{28,20},{20,12},{12,4},{4,0},{1,9},{9... | collective-permute-start | bytes 884744 | tf_op jit(solution)/shard_map/ppermute | solution.py:331
  24.1 24.8 %collective-permute-start.5 = (bf16[96,2560]{1,0:T(8,128)(2,1)S(1)}, bf16[96,2560]{1,0:T(8,128)(2,1)}, u32[]{:S(2)}, u32[]{:S(2)}) collective-permute-start(bf16[96,2560]{1,0:T(8,128)(2,1)S(1)} %collective-permute-done.3.refs_1_), channel_id=1, source_target_pairs={{0,8},{8,16},{16,24},{24,28},{28,20},{20,12},{12,4},{4,0},{1,9},{9... | collective-permute-start | bytes 1474568 | tf_op jit(solution)/shard_map/ppermute | solution.py:331
  27.3 8.9 %collective-permute-start.13 = (bf16[96,1536]{1,0:T(8,128)(2,1)S(1)}, bf16[96,1536]{1,0:T(8,128)(2,1)S(1)}, u32[]{:S(2)}, u32[]{:S(2)}) collective-permute-start(bf16[96,1536]{1,0:T(8,128)(2,1)S(1)} %collective-permute-done.11.refs_2_), channel_id=1, source_target_pairs={{8,0},{16,8},{24,16},{28,24},{20,28},{12,20},{4,12},{0,4},{9,1},{1... | collective-permute-start | bytes 884744 | tf_op jit(solution)/shard_map/ppermute | solution.py:332
  32.2 15.3 %collective-permute-start.14 = (bf16[96,1536]{1,0:T(8,128)(2,1)S(1)}, bf16[96,1536]{1,0:T(8,128)(2,1)S(1)}, u32[]{:S(2)}, u32[]{:S(2)}) collective-permute-start(bf16[96,1536]{1,0:T(8,128)(2,1)S(1)} %collective-permute-done.12.refs_3_), channel_id=1, source_target_pairs={{0,8},{8,16},{16,24},{24,28},{28,20},{20,12},{12,4},{4,0},{1,9},{9... | collective-permute-start | bytes 884744 | tf_op jit(solution)/shard_map/ppermute | solution.py:331
  34.0 22.1 %collective-permute-start.6 = (bf16[96,2560]{1,0:T(8,128)(2,1)S(1)}, bf16[96,2560]{1,0:T(8,128)(2,1)}, u32[]{:S(2)}, u32[]{:S(2)}) collective-permute-start(bf16[96,2560]{1,0:T(8,128)(2,1)S(1)} %collective-permute-done.4.refs_2_), channel_id=1, source_target_pairs={{8,0},{16,8},{24,16},{28,24},{20,28},{12,20},{4,12},{0,4},{9,1},{1... | collective-permute-start | bytes 1474568 | tf_op jit(solution)/shard_map/ppermute | solution.py:332
  36.3 42.0 %collective-permute-start.2 = (bf16[192,3328]{1,0:T(8,128)(2,1)}, bf16[192,3328]{1,0:T(8,128)(2,1)}, u32[]{:S(2)}, u32[]{:S(2)}) collective-permute-start(bf16[192,3328]{1,0:T(8,128)(2,1)} %refs_0_.1), channel_id=1, source_target_pairs={{0,1},{1,0},{2,3},{3,2},{4,5},{5,4},{6,7},{7,6},{8,9},{9,8},{10,11... | collective-permute-start | bytes 3833864 | tf_op jit(solution)/shard_map/ppermute | solution.py:367
  47.4 7.4 %collective-permute-start.15 = (bf16[96,1536]{1,0:T(8,128)(2,1)S(1)}, bf16[96,1536]{1,0:T(8,128)(2,1)S(1)}, u32[]{:S(2)}, u32[]{:S(2)}) collective-permute-start(bf16[96,1536]{1,0:T(8,128)(2,1)S(1)} %collective-permute-done.13.refs_4_), channel_id=1, source_target_pairs={{8,0},{16,8},{24,16},{28,24},{20,28},{12,20},{4,12},{0,4},{9,1},{1... | collective-permute-start | bytes 884744 | tf_op jit(solution)/shard_map/ppermute | solution.py:332
  48.9 16.0 %collective-permute-start.7 = (bf16[96,2560]{1,0:T(8,128)(2,1)}, bf16[96,2560]{1,0:T(8,128)(2,1)}, u32[]{:S(2)}, u32[]{:S(2)}) collective-permute-start(bf16[96,2560]{1,0:T(8,128)(2,1)} %collective-permute-done.5.refs_3_), channel_id=1, source_target_pairs={{0,8},{8,16},{16,24},{24,28},{28,20},{20,12},{12,4},{4,0},{1,9},{9... | collective-permute-start | bytes 1474568 | tf_op jit(solution)/shard_map/ppermute | solution.py:331
  54.8 8.5 %collective-permute-start.16 = (bf16[96,768]{1,0:T(8,128)(2,1)S(1)}, bf16[96,768]{1,0:T(8,128)(2,1)S(1)}, u32[]{:S(2)}, u32[]{:S(2)}) collective-permute-start(bf16[96,768]{1,0:T(8,128)(2,1)S(1)} %slice.16), channel_id=1, source_target_pairs={{0,8},{8,16},{16,24},{24,28},{28,20},{20,12},{12,4},{4,0},{1,9},{9... | collective-permute-start | bytes 442376 | tf_op jit(solution)/shard_map/ppermute | solution.py:336
  56.1 9.3 %collective-permute-start.17 = (bf16[96,768]{1,0:T(8,128)(2,1)S(1)}, bf16[96,768]{1,0:T(8,128)(2,1)S(1)}, u32[]{:S(2)}, u32[]{:S(2)}) collective-permute-start(bf16[96,768]{1,0:T(8,128)(2,1)S(1)} %slice.17), channel_id=1, source_target_pairs={{8,0},{16,8},{24,16},{28,24},{20,28},{12,20},{4,12},{0,4},{9,1},{1... | collective-permute-start | bytes 442376 | tf_op jit(solution)/shard_map/ppermute | solution.py:337
  63.3 17.3 %collective-permute-start.8 = (bf16[96,2560]{1,0:T(8,128)(2,1)}, bf16[96,2560]{1,0:T(8,128)(2,1)S(1)}, u32[]{:S(2)}, u32[]{:S(2)}) collective-permute-start(bf16[96,2560]{1,0:T(8,128)(2,1)} %collective-permute-done.6.refs_4_), channel_id=1, source_target_pairs={{8,0},{16,8},{24,16},{28,24},{20,28},{12,20},{4,12},{0,4},{9,1},{1... | collective-permute-start | bytes 1474568 | tf_op jit(solution)/shard_map/ppermute | solution.py:332
  64.9 36.5 %collective-permute-start.1 = (bf16[192,3328]{1,0:T(8,128)(2,1)}, bf16[192,3328]{1,0:T(8,128)(2,1)S(1)}, u32[]{:S(2)}, u32[]{:S(2)}) collective-permute-start(bf16[192,3328]{1,0:T(8,128)(2,1)} %collective-permute-done.refs_0_), channel_id=1, source_target_pairs={{0,1},{1,0},{2,3},{3,2},{4,5},{5,4},{6,7},{7,6},{8,9},{9,8},{10,11... | collective-permute-start | bytes 3833864 | tf_op jit(solution)/shard_map/ppermute | solution.py:367
  64.9 15.7 %collective-permute-start.9 = (bf16[96,2560]{1,0:T(8,128)(2,1)}, bf16[96,2560]{1,0:T(8,128)(2,1)S(1)}, u32[]{:S(2)}, u32[]{:S(2)}) collective-permute-start(bf16[96,2560]{1,0:T(8,128)(2,1)} %collective-permute-done.7.refs_5_), channel_id=1, source_target_pairs={{0,8},{8,16},{16,24},{24,28},{28,20},{20,12},{12,4},{4,0},{1,9},{9... | collective-permute-start | bytes 1474568 | tf_op jit(solution)/shard_map/ppermute | solution.py:335
  65.4 12.9 %copy-start = (bf16[192,3328]{1,0:T(8,128)(2,1)S(1)}, bf16[192,3328]{1,0:T(8,128)(2,1)}, u32[]{:S(2)}) copy-start(bf16[192,3328]{1,0:T(8,128)(2,1)} %refs_0_.1) | copy-start | bytes 3833860
  100.8 78.8 %collective-permute-start.18 = (f32[192,3328]{1,0:T(8,128)}, f32[192,3328]{1,0:T(8,128)}, u32[]{:S(2)}, u32[]{:S(2)}) collective-permute-start(f32[192,3328]{1,0:T(8,128)} %get-tuple-element.17), channel_id=1, source_target_pairs={{0,1},{1,0},{2,3},{3,2},{4,5},{5,4},{6,7},{7,6},{8,9},{9,8},{10,11... | collective-permute-start | bytes 7667720 | tf_op jit(solution)/shard_map/ppermute | solution.py:400
  101.0 43.9 %collective-permute-start.19 = (f32[192,3328]{1,0:T(8,128)S(1)}, f32[192,3328]{1,0:T(8,128)S(1)}, u32[]{:S(2)}, u32[]{:S(2)}) collective-permute-start(f32[192,3328]{1,0:T(8,128)S(1)} %get-tuple-element.19), channel_id=1, source_target_pairs={{0,1},{1,0},{2,3},{3,2},{4,5},{5,4},{6,7},{7,6},{8,9},{9,8},{10,11... | collective-permute-start | bytes 7667720 | tf_op jit(solution)/shard_map/ppermute | solution.py:397
  146.4 33.2 %collective-permute-start.20 = (bf16[192,3456]{1,0:T(8,128)(2,1)S(1)}, bf16[192,3456]{1,0:T(8,128)(2,1)S(1)}, u32[]{:S(2)}, u32[]{:S(2)}) collective-permute-start(bf16[192,3456]{1,0:T(8,128)(2,1)S(1)} %encode.1), channel_id=1, source_target_pairs={{0,2},{1,3},{2,0},{3,1},{4,6},{5,7},{6,4},{7,5},{8,10},{9,11},{10,... | collective-permute-start | bytes 3981320 | tf_op jit(solution)/shard_map/ppermute | solution.py:399
